TPU v7x, 32 devices: a whole 2x2x4 slice. The times are simulated.
32 devices in a mesh: dp: 16 (over z, x, core), ctx: 2 (over y).
Axes of the slice: x: 2, y: 2, z: 4, core: 2. Of those that a mesh axis runs over, the one named last changes fastest.
Arguments:
- block_input: bfloat16 [16, 256, 768], P('dp', 'ctx'), may hold values from -6 to 6
- out_grad: bfloat16 [16, 256, 768], P('dp', 'ctx'), may hold values from -6 to 6
- positions: int32 [16, 256], P('dp', 'ctx'), may hold values from 0 to 255, as said below
- w_qkv: float32 [768, 2304], P('dp'), may hold values from -0.3125 to 0.3125
- w_attn_out: float32 [768, 768], P('dp'), may hold values from -0.625 to 0.625
- w_in: float32 [768, 2304], P('dp'), may hold values from -0.21875 to 0.21875
- w_mlp_out: float32 [768, 1152], P('dp'), may hold values from -0.1875 to 0.1875
- norm_gains: float32 [2, 768], P(None, 'dp'), may hold values from 0.5 to 1.5
- m_qkv: float32 [768, 2304], P('dp'), may hold values from -0.9 to 0.9
- m_attn_out: float32 [768, 768], P('dp'), may hold values from -0.9 to 0.9
- m_in: float32 [768, 2304], P('dp'), may hold values from -0.9 to 0.9
- m_mlp_out: float32 [768, 1152], P('dp'), may hold values from -0.9 to 0.9
- gain_mean: float32 [2, 768], P(None, 'dp'), may hold values from -0.3 to 0.3
- gain_var: float32 [2, 768], P(None, 'dp'), may hold values from 0.05 to 0.5
Outputs:
- block_output: bfloat16 [16, 256, 768], P('dp', 'ctx')
- input_grad: float32 [16, 256, 768], P('dp', 'ctx')
- grad_qkv: float32 [768, 2304], P('dp')
- grad_attn_out: float32 [768, 768], P('dp')
- grad_in: float32 [768, 2304], P('dp')
- grad_mlp_out: float32 [768, 1152], P('dp')
- grad_gains: float32 [2, 768], P(None, 'dp')
- new_qkv: float32 [768, 2304], P('dp')
- new_attn_out: float32 [768, 768], P('dp')
- new_in: float32 [768, 2304], P('dp')
- new_mlp_out: float32 [768, 1152], P('dp')
- new_gains: float32 [2, 768], P(None, 'dp')
- new_m_qkv: float32 [768, 2304], P('dp')
- new_m_attn_out: float32 [768, 768], P('dp')
- new_m_in: float32 [768, 2304], P('dp')
- new_m_mlp_out: float32 [768, 1152], P('dp')
- new_gain_mean: float32 [2, 768], P(None, 'dp')
- new_gain_var: float32 [2, 768], P(None, 'dp')
Inputs may be any that keep to these rules, and one draw needn't show every extreme that they name: In each sequence positions count up by one and restart at 0 at the first token of each packed document; every sequence begins at 0; documents vary in length and number; the first sequence is a single document.
All inputs are finite; a program needn't handle non-finite values.
Results may differ from a plain program's by a relative error of at most 0.035.
Values may be sent and summed in bfloat16 or wider, within the bound.
No kernel may reach another device: no remote copies, remote signals or barrier semaphores. Data moves between devices by JAX's collectives and lax.ppermute only.
A program may use at most 128 MiB of HBM per device.

v0:
```python
import math

import jax
import jax.numpy as jnp
from jax import lax
from jax.sharding import PartitionSpec as P

HEADS = 12
NS_ITERS = 5


theta_base = 160000.0
norm_eps = 1e-05
quintic_one = 3.4445
quintic_two = -4.775
quintic_three = 2.0315
momentum_rate = 0.95
matrix_rate = 0.04
gain_rate = 0.1
beta_first = 0.9
beta_second = 0.95
adam_eps = 1e-08
first_fix = 1.0 - 0.9**10
second_fix = 1.0 - 0.95**10
ortho_eps = 1e-07


def shortened(value):
    return jax.tree.map(lambda a: a.astype(jnp.bfloat16) if a.dtype == jnp.float32 else a, value)


def rope_tables(positions, head_size):
    half_size = head_size // 2
    indices = jnp.arange(half_size, dtype=jnp.float32)
    frequency = jnp.exp(indices * (-2.0 * math.log(theta_base) / head_size))
    angles = positions.astype(jnp.float32)[:, None] * frequency[None, :]
    return (jnp.cos(angles)[:, None, :], jnp.sin(angles)[:, None, :])


def rotate(field, cosine, sine):
    half_size = field.shape[-1] // 2
    first_half = field[..., :half_size]
    second_half = field[..., half_size:]
    return jnp.concatenate(
        [first_half * cosine - second_half * sine, second_half * cosine + first_half * sine],
        axis=-1,
    )


def rotate_back(gradient, cosine, sine):
    half_size = gradient.shape[-1] // 2
    first_half = gradient[..., :half_size]
    second_half = gradient[..., half_size:]
    return jnp.concatenate(
        [first_half * cosine + second_half * sine, second_half * cosine - first_half * sine],
        axis=-1,
    )


def normalize(field):
    centered = field - jnp.mean(field, axis=-1, keepdims=True)
    factor = lax.rsqrt(jnp.mean(centered * centered, axis=-1, keepdims=True) + norm_eps)
    return (centered * factor, factor)


def normalize_back(grad_hat, normed, factor):
    first_mean = jnp.mean(grad_hat, axis=-1, keepdims=True)
    second_mean = jnp.mean(grad_hat * normed, axis=-1, keepdims=True)
    return factor * (grad_hat - first_mean - normed * second_mean)


def gelu_parts(preact):
    cumulative = 0.5 * (1.0 + lax.erf(preact * (1.0 / math.sqrt(2.0))))
    activated = preact * cumulative
    derivative = cumulative + preact * jnp.exp(-0.5 * preact * preact) * (
        1.0 / math.sqrt(2.0 * math.pi)
    )
    return (activated, derivative)


def contract_rows(left_side, right_side):
    return lax.dot_general(
        left_side, right_side, (((0,), (0,)), ((), ())), preferred_element_type=jnp.float32
    )


def contract_cols(left_side, right_side):
    return lax.dot_general(
        left_side, right_side, (((1,), (1,)), ((), ())), preferred_element_type=jnp.float32
    )


def pair_terms(
    query_heads,
    grad_heads,
    delta_rows,
    log_rows,
    query_docs,
    key_heads,
    value_heads,
    key_docs,
    score_scale,
):
    f32 = jnp.float32
    scores = (
        jnp.einsum("qhd,khd->hqk", query_heads, key_heads, preferred_element_type=f32) * score_scale
    )
    same = (query_docs[:, None] == key_docs[None, :])[None]
    probs = jnp.where(same, jnp.exp(scores - log_rows[:, :, None]), 0.0)
    grad_probs = jnp.einsum("qhd,khd->hqk", grad_heads, value_heads, preferred_element_type=f32)
    grad_scores_b = (probs * (grad_probs - jnp.transpose(delta_rows)[:, :, None])).astype(
        jnp.bfloat16
    )
    return (probs.astype(jnp.bfloat16), grad_scores_b)


def gram_of(iterate):
    highest = lax.Precision.HIGHEST
    owned_rows = iterate.shape[0] // lax.axis_size("ctx")
    picked = lax.slice_in_dim(iterate, 0, owned_rows * lax.axis_size("ctx"), axis=0)
    gram_share = lax.psum_scatter(
        jnp.dot(picked, iterate.T, precision=highest, preferred_element_type=jnp.float32).astype(
            jnp.bfloat16
        ),
        "ctx",
        scatter_dimension=0,
        tiled=True,
    ).astype(jnp.float32)
    return lax.all_gather(gram_share.astype(jnp.bfloat16), "ctx", axis=0, tiled=True).astype(
        gram_share.dtype
    )


def orthogonalize(moment):
    highest = lax.Precision.HIGHEST
    gram_matrix = gram_of(moment)
    inverse = 1.0 / (jnp.sqrt(jnp.trace(gram_matrix)) + ortho_eps)
    iterate = moment * inverse
    gram_matrix = gram_matrix * (inverse * inverse)
    for sweep_index in range(NS_ITERS):
        first_product = jnp.dot(gram_matrix, iterate, precision=highest)
        second_product = jnp.dot(gram_matrix, first_product, precision=highest)
        iterate = (
            quintic_one * iterate + quintic_two * first_product + quintic_three * second_product
        )
        if sweep_index + 1 < NS_ITERS:
            gram_matrix = gram_of(iterate)
    return iterate


def per_device(
    block_input,
    out_grad,
    positions,
    w_qkv,
    w_attn_out,
    w_in,
    w_mlp_out,
    norm_gains,
    m_qkv,
    m_attn_out,
    m_in,
    m_mlp_out,
    gain_mean,
    gain_var,
):
    bf16 = jnp.bfloat16
    f32 = jnp.float32
    dp_count = lax.axis_size("dp")
    ctx_count = lax.axis_size("ctx")
    tok_rows = block_input.shape[1]
    width = block_input.shape[2]
    heads = HEADS
    head_size = width // heads
    score_scale = 1.0 / math.sqrt(head_size)
    seq_length = tok_rows * ctx_count
    key_block = math.gcd(seq_length, 512)
    block_count = seq_length // key_block
    gathered = (
        lax.all_gather(w_qkv.astype(bf16), "dp", axis=0, tiled=True),
        lax.all_gather(w_attn_out.astype(bf16), "dp", axis=0, tiled=True),
        lax.all_gather(w_in.astype(bf16), "dp", axis=0, tiled=True),
        lax.all_gather(w_mlp_out.astype(bf16), "dp", axis=0, tiled=True),
        lax.all_gather(norm_gains.astype(bf16), "dp", axis=1, tiled=True),
    )
    w_qkv_b, w_out_b, w_in_b, w_mlp_b, gains_b = gathered
    gain_one = gains_b[0].astype(f32)
    gain_two = gains_b[1].astype(f32)
    x_wide = block_input[0].astype(f32)
    dy_seq = out_grad[0]
    hat_one, factor_one = normalize(x_wide)
    act_one = (hat_one * gain_one).astype(bf16)
    qkv = jnp.dot(act_one, w_qkv_b, preferred_element_type=f32)
    cosine, sine = rope_tables(positions[0], head_size)
    doc_own = (
        lax.axis_index("ctx") * tok_rows + jnp.arange(tok_rows, dtype=jnp.int32) - positions[0]
    )
    queries_b = rotate(qkv[:, :width].reshape(tok_rows, heads, head_size), cosine, sine).astype(
        bf16
    )
    keys_flat = (
        rotate(qkv[:, width : 2 * width].reshape(tok_rows, heads, head_size), cosine, sine)
        .astype(bf16)
        .reshape(tok_rows, width)
    )
    values_flat = qkv[:, 2 * width :].astype(bf16)
    key_piece = lax.all_gather(keys_flat, "ctx", axis=0, tiled=True)
    value_piece = lax.all_gather(values_flat, "ctx", axis=0, tiled=True)
    doc_piece = lax.all_gather(doc_own, "ctx", axis=0, tiled=True)
    rows_here = key_piece.shape[0]
    key_heads = key_piece.reshape(rows_here, heads, head_size)
    value_heads = value_piece.reshape(rows_here, heads, head_size)
    scores = (
        jnp.einsum("qhd,khd->hqk", queries_b, key_heads, preferred_element_type=f32) * score_scale
    )
    same = (doc_own[:, None] == doc_piece[None, :])[None]
    weights = jnp.where(same, jnp.exp(scores), 0.0)
    totals = jnp.sum(weights, axis=-1)
    summed = jnp.einsum(
        "hqk,khd->qhd", weights.astype(bf16), value_heads, preferred_element_type=f32
    )
    fold_result = (summed, totals)
    summed_values, total_weights = fold_result
    attended = summed_values / jnp.transpose(total_weights)[:, :, None]
    log_total = jnp.log(total_weights)
    mixed_b = attended.reshape(tok_rows, width).astype(bf16)
    hidden = x_wide + jnp.dot(mixed_b, w_out_b, preferred_element_type=f32)
    hat_two, factor_two = normalize(hidden)
    act_two = (hat_two * gain_two).astype(bf16)
    lifted = jnp.dot(act_two, w_in_b, preferred_element_type=f32)
    hidden_units = lifted.shape[1] // 2
    preact = lifted[:, :hidden_units]
    gate_half = lifted[:, hidden_units:]
    activated, derivative = gelu_parts(preact)
    inner_b = (activated * gate_half).astype(bf16)
    output = hidden + contract_cols(inner_b, w_mlp_b)
    dy_wide = dy_seq.astype(f32)
    grad_mlp = contract_rows(dy_seq, inner_b)
    grad_inner = jnp.dot(dy_seq, w_mlp_b, preferred_element_type=f32)
    grad_lift = jnp.concatenate(
        [grad_inner * gate_half * derivative, grad_inner * activated], axis=1
    ).astype(bf16)
    grad_in = contract_rows(act_two, grad_lift)
    grad_act_two = contract_cols(grad_lift, w_in_b)
    gain_grad_two = jnp.sum(grad_act_two * hat_two, axis=0)
    grad_hidden = dy_wide + normalize_back(grad_act_two * gain_two, hat_two, factor_two)
    grad_hidden_b = grad_hidden.astype(bf16)
    grad_out = contract_rows(mixed_b, grad_hidden_b)
    grad_mixed = contract_cols(grad_hidden_b, w_out_b).reshape(tok_rows, heads, head_size)
    delta = jnp.sum(grad_mixed * attended, axis=-1)
    grad_mixed_b = grad_mixed.astype(bf16)
    keys_all, values_all, docs_all = (
        lax.all_gather(keys_flat, "ctx", axis=0, tiled=True),
        lax.all_gather(values_flat, "ctx", axis=0, tiled=True),
        lax.all_gather(doc_own, "ctx", axis=0, tiled=True),
    )
    key_pieces = (
        keys_all.reshape(block_count, key_block, width),
        values_all.reshape(block_count, key_block, width),
        docs_all.reshape(block_count, key_block),
    )
    zero_query = jnp.zeros((tok_rows, heads, head_size), f32)

    def query_only_step(query_grad, pieces):
        key_piece, value_piece, doc_piece = pieces
        key_heads = key_piece.reshape(key_block, heads, head_size)
        value_heads = value_piece.reshape(key_block, heads, head_size)
        probs_b, grad_scores_b = pair_terms(
            queries_b,
            grad_mixed_b,
            delta,
            log_total,
            doc_own,
            key_heads,
            value_heads,
            doc_piece,
            score_scale,
        )
        query_grad = (
            query_grad
            + jnp.einsum("hqk,khd->qhd", grad_scores_b, key_heads, preferred_element_type=f32)
            * score_scale
        )
        return (query_grad, None)

    query_grad, unused_terms = lax.scan(query_only_step, zero_query, key_pieces)
    queries_all, grads_all, logs_all, deltas_all, qdocs_all = (
        lax.all_gather(queries_b.reshape(tok_rows, width), "ctx", axis=0, tiled=True),
        lax.all_gather(grad_mixed_b.reshape(tok_rows, width), "ctx", axis=0, tiled=True),
        lax.all_gather(log_total.astype(jnp.bfloat16), "ctx", axis=1, tiled=True).astype(
            log_total.dtype
        ),
        lax.all_gather(delta.astype(jnp.bfloat16), "ctx", axis=0, tiled=True).astype(delta.dtype),
        lax.all_gather(doc_own, "ctx", axis=0, tiled=True),
    )
    own_keys = keys_flat.reshape(tok_rows, heads, head_size)
    own_values = values_flat.reshape(tok_rows, heads, head_size)

    def key_side_step(carry, pieces):
        key_acc, value_acc = carry
        query_piece, grad_piece, log_piece, delta_piece, qdoc_piece = pieces
        query_heads = query_piece.reshape(key_block, heads, head_size)
        grad_heads = grad_piece.reshape(key_block, heads, head_size)
        probs_b, grad_scores_b = pair_terms(
            query_heads,
            grad_heads,
            delta_piece,
            log_piece,
            qdoc_piece,
            own_keys,
            own_values,
            doc_own,
            score_scale,
        )
        value_acc = value_acc + jnp.einsum(
            "hqk,qhd->khd", probs_b, grad_heads, preferred_element_type=f32
        )
        key_acc = (
            key_acc
            + jnp.einsum("hqk,qhd->khd", grad_scores_b, query_heads, preferred_element_type=f32)
            * score_scale
        )
        return ((key_acc, value_acc), None)

    query_pieces = (
        queries_all.reshape(block_count, key_block, width),
        grads_all.reshape(block_count, key_block, width),
        jnp.transpose(logs_all.reshape(heads, block_count, key_block), (1, 0, 2)),
        deltas_all.reshape(block_count, key_block, heads),
        qdocs_all.reshape(block_count, key_block),
    )
    (key_acc, value_acc), unused_side = lax.scan(
        key_side_step, (zero_query, zero_query), query_pieces
    )
    key_grad = key_acc.reshape(tok_rows, width)
    value_grad = value_acc.reshape(tok_rows, width)
    grad_qkv_in = jnp.concatenate(
        [
            rotate_back(query_grad, cosine, sine).reshape(tok_rows, width),
            rotate_back(key_grad.reshape(tok_rows, heads, head_size), cosine, sine).reshape(
                tok_rows, width
            ),
            value_grad,
        ],
        axis=1,
    ).astype(bf16)
    grad_qkv = contract_rows(act_one, grad_qkv_in)
    grad_act_one = contract_cols(grad_qkv_in, w_qkv_b)
    gain_grad_one = jnp.sum(grad_act_one * hat_one, axis=0)
    grad_input = grad_hidden + normalize_back(grad_act_one * gain_one, hat_one, factor_one)
    gain_grads = jnp.stack([gain_grad_one, gain_grad_two])
    shares = (
        lax.psum_scatter(
            grad_qkv.astype(jnp.bfloat16), "dp", scatter_dimension=0, tiled=True
        ).astype(jnp.float32),
        lax.psum_scatter(
            grad_out.astype(jnp.bfloat16), "dp", scatter_dimension=0, tiled=True
        ).astype(jnp.float32),
        lax.psum_scatter(
            grad_in.astype(jnp.bfloat16), "dp", scatter_dimension=0, tiled=True
        ).astype(jnp.float32),
        lax.psum_scatter(
            grad_mlp.astype(jnp.bfloat16), "dp", scatter_dimension=0, tiled=True
        ).astype(jnp.float32),
        lax.psum_scatter(
            gain_grads.astype(jnp.bfloat16), "dp", scatter_dimension=1, tiled=True
        ).astype(jnp.float32),
    )
    summed_grads = (
        lax.psum(shares[0].astype(jnp.bfloat16), "ctx").astype(jnp.float32),
        lax.psum(shares[1].astype(jnp.bfloat16), "ctx").astype(jnp.float32),
        lax.psum(shares[2].astype(jnp.bfloat16), "ctx").astype(jnp.float32),
        lax.psum(shares[3].astype(jnp.bfloat16), "ctx").astype(jnp.float32),
        lax.psum(shares[4].astype(jnp.bfloat16), "ctx").astype(jnp.float32),
    )
    factor = 1.0 / math.sqrt(dp_count * ctx_count * tok_rows)
    grads = [total * factor for total in summed_grads]
    matrices = (w_qkv, w_attn_out, w_in, w_mlp_out)
    moments = (m_qkv, m_attn_out, m_in, m_mlp_out)
    moments_next = [momentum_rate * moment + grad for moment, grad in zip(moments, grads[:4])]
    owned_rows = w_qkv.shape[0]
    widest = max(w_qkv.shape[1], w_in.shape[1])
    col_count = widest // ctx_count
    ctx_place = lax.axis_index("ctx")

    def owner_slice(matrix):
        padded = jnp.pad(matrix, ((0, 0), (0, widest - matrix.shape[1])))
        return lax.dynamic_slice_in_dim(padded, ctx_place * col_count, col_count, 1)

    filled_slots = jnp.stack([owner_slice(moment) for moment in moments_next])
    empty_slots = jnp.zeros((dp_count - 4, owned_rows, col_count), f32)
    send_buffer = jnp.concatenate([filled_slots, empty_slots], axis=0)
    received = lax.all_to_all(
        send_buffer.astype(jnp.bfloat16), "dp", split_axis=0, concat_axis=0, tiled=True
    ).astype(send_buffer.dtype)
    owned_matrix = received.reshape(dp_count * owned_rows, col_count)
    orthogonal = orthogonalize(owned_matrix)
    returned = lax.all_to_all(
        shortened(orthogonal.reshape(dp_count, owned_rows, col_count)),
        "dp",
        split_axis=0,
        concat_axis=0,
        tiled=True,
    )
    updates = lax.all_gather(shortened(returned[:4]), "ctx", axis=2, tiled=True)
    new_weights = []
    for slot_index in range(4):
        weight = matrices[slot_index]
        full_rows = weight.shape[0] * dp_count
        rate = matrix_rate * math.sqrt(max(full_rows, weight.shape[1]))
        new_weights.append(weight - rate * updates[slot_index][:, : weight.shape[1]])
    gain_grad = grads[4]
    mean_next = beta_first * gain_mean + (1.0 - beta_first) * gain_grad
    var_next = beta_second * gain_var + (1.0 - beta_second) * gain_grad * gain_grad
    gains_next = norm_gains - gain_rate * (mean_next / first_fix) / (
        jnp.sqrt(var_next / second_fix) + adam_eps
    )
    return (
        output.astype(bf16)[None],
        grad_input[None],
        grads[0],
        grads[1],
        grads[2],
        grads[3],
        gain_grad,
        new_weights[0],
        new_weights[1],
        new_weights[2],
        new_weights[3],
        gains_next,
        moments_next[0],
        moments_next[1],
        moments_next[2],
        moments_next[3],
        mean_next,
        var_next,
    )


def solution(mesh):
    placed = (
        P("dp", "ctx", None),
        P("dp", "ctx", None),
        P("dp", "ctx"),
        P("dp", None),
        P("dp", None),
        P("dp", None),
        P("dp", None),
        P(None, "dp"),
        P("dp", None),
        P("dp", None),
        P("dp", None),
        P("dp", None),
        P(None, "dp"),
        P(None, "dp"),
    )
    return jax.shard_map(
        per_device,
        mesh=mesh,
        in_specs=placed,
        out_specs=(
            P("dp", "ctx", None),
            P("dp", "ctx", None),
            P("dp", None),
            P("dp", None),
            P("dp", None),
            P("dp", None),
            P(None, "dp"),
            P("dp", None),
            P("dp", None),
            P("dp", None),
            P("dp", None),
            P(None, "dp"),
            P("dp", None),
            P("dp", None),
            P("dp", None),
            P("dp", None),
            P(None, "dp"),
            P(None, "dp"),
        ),
        check_vma=False,
    )
```

profile of v0, /device:TPU:26, one launch (start us, length us, event | category | flops | bytes accessed | tf_op | source)
XLA Modules:
  0.0 999.2 jit_solution(11891595801324001571)
XLA Ops:
  14.8 16.7 %all-gather = bf16[16,48,2]{1,2,0:T(2,128)(2,1)S(1)} all-gather(bf16[1,48,2]{1,2,0:T(2,128)(2,1)S(1)} %convert_bitcast_fusion.2), channel_id=1, replica_groups=mesh['dp'=16,'ctx'=2] {'dp'}, dimensions={0}, use_global_device_ids=true | all-gather | bytes 3264 | tf_op jit(solution)/shard_map/all_gather | solution.py:184
  36.0 20.7 %all-gather.12.cloned.1.call-done = bf16[768,2304]{1,0:T(8,128)(2,1)} async-done(((bf16[48,2304]{1,0:T(8,128)(2,1)}), bf16[768,2304]{1,0:T(8,128)(2,1)}) %all-gather.12.cloned.1.call-update) | async-done | bytes 3538960 | tf_op jit(solution)/shard_map/all_gather | solution.py:180
  78.5 18.3 %all-gather.14.cloned.1.call-done = bf16[768,768]{1,0:T(8,128)(2,1)} async-done(((bf16[48,768]{1,0:T(8,128)(2,1)}), bf16[768,768]{1,0:T(8,128)(2,1)}) %all-gather.14.cloned.1.call-update) | async-done | bytes 1179664 | tf_op jit(solution)/shard_map/all_gather | solution.py:181
  98.8 46.7 %all-gather.16.cloned.1.call-done = bf16[768,2304]{1,0:T(8,128)(2,1)} async-done(((bf16[48,2304]{1,0:T(8,128)(2,1)}), bf16[768,2304]{1,0:T(8,128)(2,1)}) %all-gather.16.cloned.1.call-update) | async-done | bytes 3538960 | tf_op jit(solution)/shard_map/all_gather | solution.py:182
  148.2 39.0 %all-gather.18.cloned.1.call-done = bf16[768,1152]{1,0:T(8,128)(2,1)} async-done(((bf16[48,1152]{1,0:T(8,128)(2,1)}), bf16[768,1152]{1,0:T(8,128)(2,1)}) %all-gather.18.cloned.1.call-update) | async-done | bytes 1769488 | tf_op jit(solution)/shard_map/all_gather | solution.py:183
  253.4 59.0 %reduce-scatter.17.cloned.1.call-done = bf16[48,768]{1,0:T(8,128)(2,1)} async-done(((bf16[768,768]{1,0:T(8,128)(2,1)}), bf16[48,768]{1,0:T(8,128)(2,1)}) %reduce-scatter.17.cloned.1.call-update) | async-done | bytes 73744 | tf_op jit(solution)/shard_map/reduce_scatter | solution.py:356
  312.4 70.7 %reduce-scatter.15.cloned.1.call-done = bf16[48,2304]{1,0:T(8,128)(2,1)} async-done(((bf16[768,2304]{1,0:T(8,128)(2,1)}), bf16[48,2304]{1,0:T(8,128)(2,1)}) %reduce-scatter.15.cloned.1.call-update) | async-done | bytes 221200 | tf_op jit(solution)/shard_map/reduce_scatter | solution.py:353
  383.0 71.1 %reduce-scatter.19.cloned.1.call-done = bf16[48,2304]{1,0:T(8,128)(2,1)} async-done(((bf16[768,2304]{1,0:T(8,128)(2,1)}), bf16[48,2304]{1,0:T(8,128)(2,1)}) %reduce-scatter.19.cloned.1.call-update) | async-done | bytes 221200 | tf_op jit(solution)/shard_map/reduce_scatter | solution.py:359
  454.5 38.7 %all-reduce.5.cloned.1.call-done = (bf16[48,2304]{1,0:T(8,128)(2,1)}, bf16[48,768]{1,0:T(8,128)(2,1)}, bf16[48,2304]{1,0:T(8,128)(2,1)}, bf16[48,1152]{0,1:T(8,128)(2,1)}) async-done(((bf16[48,2304]{1,0:T(8,128)(2,1)}, bf16[48,768]{1,0:T(8,128)(2,1)}, bf16[48,2304]{1,0:T(8,128)(2,1)}, bf16[48,1152]{0,1:T(8,128)(2,1)}), (bf16[48,2304]{1,0:T(8,128)(2,1)}, bf16[48,768]{1,0:T(8,128)(2,1)}, ...) | async-done | bytes 626704 | tf_op jit(solution)/shard_map/psum | solution.py:370
  501.8 45.1 %all_to_all.10 = bf16[16,48,1152]{2,1,0:T(8,128)(2,1)S(1)} all-to-all(bf16[16,48,1152]{2,1,0:T(8,128)(2,1)S(1)} %broadcast_dynamic-update-slice_fusion), channel_id=1, replica_groups=mesh['dp'=16,'ctx'=2] {'dp'}, dimensions={0} | all-to-all | bytes 3538944 | tf_op jit(solution)/shard_map/all_to_all | solution.py:393
  549.7 22.1 %reduce-scatter.21.cloned.1.call-done = bf16[384,768]{1,0:T(8,128)(2,1)} async-done(((bf16[768,768]{1,0:T(8,128)(2,1)}), bf16[384,768]{1,0:T(8,128)(2,1)}) %reduce-scatter.21.cloned.1.call-update) | async-done | bytes 589840 | tf_op jit(solution)/shard_map/reduce_scatter | solution.py:121
  572.1 24.1 %all-gather.20.cloned.1.call-done = bf16[768,768]{1,0:T(8,128)(2,1)} async-done(((bf16[384,768]{1,0:T(8,128)(2,1)}), bf16[768,768]{1,0:T(8,128)(2,1)}) %all-gather.20.cloned.1.call-update) | async-done | bytes 1179664 | tf_op jit(solution)/shard_map/all_gather | solution.py:129
  631.5 21.9 %reduce-scatter.23.cloned.1.call-done = bf16[384,768]{1,0:T(8,128)(2,1)} async-done(((bf16[768,768]{1,0:T(8,128)(2,1)}), bf16[384,768]{1,0:T(8,128)(2,1)}) %reduce-scatter.23.cloned.1.call-update) | async-done | bytes 589840 | tf_op jit(solution)/shard_map/reduce_scatter | solution.py:121
  653.5 24.3 %all-gather.22.cloned.1.call-done = bf16[768,768]{1,0:T(8,128)(2,1)} async-done(((bf16[384,768]{1,0:T(8,128)(2,1)}), bf16[768,768]{1,0:T(8,128)(2,1)}) %all-gather.22.cloned.1.call-update) | async-done | bytes 1179664 | tf_op jit(solution)/shard_map/all_gather | solution.py:129
  691.4 11.0 %convolution_convert_fusion.5 = bf16[768,768]{1,0:T(8,128)(2,1)} fusion(f32[768,1152]{1,0:T(8,128)S(1)} %fusion.1), kind=kOutput, calls=%fused_computation.27 | convolution fusion | flops 8154316800 | bytes 4718592 | tf_op jit(solution)/shard_map/dot_general | solution.py:122
  702.5 21.9 %reduce-scatter.25.cloned.1.call-done = bf16[384,768]{1,0:T(8,128)(2,1)} async-done(((bf16[768,768]{1,0:T(8,128)(2,1)}), bf16[384,768]{1,0:T(8,128)(2,1)}) %reduce-scatter.25.cloned.1.call-update) | async-done | bytes 589840 | tf_op jit(solution)/shard_map/reduce_scatter | solution.py:121
  724.9 23.7 %all-gather.24.cloned.1.call-done = bf16[768,768]{1,0:T(8,128)(2,1)} async-done(((bf16[384,768]{1,0:T(8,128)(2,1)}), bf16[768,768]{1,0:T(8,128)(2,1)}) %all-gather.24.cloned.1.call-update) | async-done | bytes 1179664 | tf_op jit(solution)/shard_map/all_gather | solution.py:129
  763.3 11.0 %convolution_convert_fusion.4 = bf16[768,768]{1,0:T(8,128)(2,1)} fusion(f32[768,1152]{1,0:T(8,128)S(1)} %fusion.2), kind=kOutput, calls=%fused_computation.26 | convolution fusion | flops 8154316800 | bytes 4718592 | tf_op jit(solution)/shard_map/dot_general | solution.py:122
  774.3 21.9 %reduce-scatter.27.cloned.1.call-done = bf16[384,768]{1,0:T(8,128)(2,1)} async-done(((bf16[768,768]{1,0:T(8,128)(2,1)}), bf16[384,768]{1,0:T(8,128)(2,1)}) %reduce-scatter.27.cloned.1.call-update) | async-done | bytes 589840 | tf_op jit(solution)/shard_map/reduce_scatter | solution.py:121
  796.5 23.9 %all-gather.26.cloned.1.call-done = bf16[768,768]{1,0:T(8,128)(2,1)} async-done(((bf16[384,768]{1,0:T(8,128)(2,1)}), bf16[768,768]{1,0:T(8,128)(2,1)}) %all-gather.26.cloned.1.call-update) | async-done | bytes 1179664 | tf_op jit(solution)/shard_map/all_gather | solution.py:129
  835.1 11.2 %convolution_convert_fusion.3 = bf16[768,768]{1,0:T(8,128)(2,1)} fusion(f32[768,1152]{1,0:T(8,128)S(1)} %fusion.3), kind=kOutput, calls=%fused_computation.25 | convolution fusion | flops 8154316800 | bytes 4718592 | tf_op jit(solution)/shard_map/dot_general | solution.py:122
  846.5 21.8 %reduce-scatter.29.cloned.1.call-done = bf16[384,768]{1,0:T(8,128)(2,1)} async-done(((bf16[768,768]{1,0:T(8,128)(2,1)}), bf16[384,768]{1,0:T(8,128)(2,1)}) %reduce-scatter.29.cloned.1.call-update) | async-done | bytes 589840 | tf_op jit(solution)/shard_map/reduce_scatter | solution.py:121
  868.4 24.3 %all-gather.28.cloned.1.call-done = bf16[768,768]{1,0:T(8,128)(2,1)} async-done(((bf16[384,768]{1,0:T(8,128)(2,1)}), bf16[768,768]{1,0:T(8,128)(2,1)}) %all-gather.28.cloned.1.call-update) | async-done | bytes 1179664 | tf_op jit(solution)/shard_map/all_gather | solution.py:129
  923.1 46.8 %reduce-scatter.33.cloned.1.call-done = bf16[48,2]{1,0:T(8,128)(2,1)} async-done(((bf16[768,2]{1,0:T(8,128)(2,1)}), bf16[48,2]{1,0:T(8,128)(2,1)}) %reduce-scatter.33.cloned.1.call-update) | async-done | bytes 208
  (299 shorter events, 247.0 us)
Async XLA Ops:
  7.2 49.5 %all-gather.12.cloned.1.call-start = ((), (), s32[]{:S(2)}) async-start(), calls=%async_computation.12 | async-start | bytes 3760128 | tf_op jit(solution)/shard_map/all_gather | solution.py:180
  9.1 87.7 %all-gather.14.cloned.1.call-start = ((), (), s32[]{:S(2)}) async-start(), calls=%async_computation.13 | async-start | bytes 1253376 | tf_op jit(solution)/shard_map/all_gather | solution.py:181
  10.7 134.7 %all-gather.16.cloned.1.call-start = ((), (), s32[]{:S(2)}) async-start(), calls=%async_computation.14 | async-start | bytes 3760128 | tf_op jit(solution)/shard_map/all_gather | solution.py:182
  12.5 174.6 %all-gather.18.cloned.1.call-start = ((), (), s32[]{:S(2)}) async-start(), calls=%async_computation.15 | async-start | bytes 1880064 | tf_op jit(solution)/shard_map/all_gather | solution.py:183
  14.2 237.4 %reduce-scatter.31.cloned.1.call-start = ((), (), s32[]{:S(2)}) async-start(), calls=%async_computation.29 | async-start | bytes 1880064
  98.5 139.8 %copy-start.4 = (f32[128,768]{1,0:T(8,128)}, f32[128,768]{1,0:T(8,128)S(1)}, u32[]{:S(2)}) copy-start(f32[128,768]{1,0:T(8,128)S(1)} %get-tuple-element.191) | copy-start | bytes 1179652
  193.6 118.8 %reduce-scatter.17.cloned.1.call-start = ((), (), s32[]{:S(2)}) async-start(), calls=%async_computation.17 | async-start | bytes 1253376 | tf_op jit(solution)/shard_map/reduce_scatter | solution.py:356
  218.9 164.1 %reduce-scatter.15.cloned.1.call-start = ((), (), s32[]{:S(2)}) async-start(), calls=%async_computation.16 | async-start | bytes 3760128 | tf_op jit(solution)/shard_map/reduce_scatter | solution.py:353
  238.3 215.9 %reduce-scatter.19.cloned.1.call-start = ((), (), s32[]{:S(2)}) async-start(), calls=%async_computation.18 | async-start | bytes 3760128 | tf_op jit(solution)/shard_map/reduce_scatter | solution.py:359
  242.4 211.9 %copy-start.47 = (f32[48,1152]{1,0:T(8,128)S(1)}, f32[48,1152]{1,0:T(8,128)}, u32[]{:S(2)}) copy-start(f32[48,1152]{1,0:T(8,128)} %param.25) | copy-start | bytes 663556
  242.4 250.9 %copy-start.34 = (f32[48,2304]{1,0:T(8,128)S(1)}, f32[48,2304]{1,0:T(8,128)}, u32[]{:S(2)}) copy-start(f32[48,2304]{1,0:T(8,128)} %param.22) | copy-start | bytes 1327108
  242.4 250.8 %all-reduce.5.cloned.1.call-start = ((), (), s32[]{:S(2)}) async-start(), calls=%async_computation.31 | async-start | bytes 1622016 | tf_op jit(solution)/shard_map/psum | solution.py:370
  454.2 117.6 %reduce-scatter.21.cloned.1.call-start = ((), (), s32[]{:S(2)}) async-start(), calls=%async_computation.19 | async-start | bytes 1769472 | tf_op jit(solution)/shard_map/reduce_scatter | solution.py:121
  549.6 46.5 %all-gather.20.cloned.1.call-start = ((), (), s32[]{:S(2)}) async-start(), calls=%async_computation.20 | async-start | bytes 1769472 | tf_op jit(solution)/shard_map/all_gather | solution.py:129
  571.8 81.6 %reduce-scatter.23.cloned.1.call-start = ((), (), s32[]{:S(2)}) async-start(), calls=%async_computation.21 | async-start | bytes 1769472 | tf_op jit(solution)/shard_map/reduce_scatter | solution.py:121
  631.5 46.3 %all-gather.22.cloned.1.call-start = ((), (), s32[]{:S(2)}) async-start(), calls=%async_computation.22 | async-start | bytes 1769472 | tf_op jit(solution)/shard_map/all_gather | solution.py:129
  653.5 70.9 %reduce-scatter.25.cloned.1.call-start = ((), (), s32[]{:S(2)}) async-start(), calls=%async_computation.23 | async-start | bytes 1769472 | tf_op jit(solution)/shard_map/reduce_scatter | solution.py:121
  702.4 46.2 %all-gather.24.cloned.1.call-start = ((), (), s32[]{:S(2)}) async-start(), calls=%async_computation.24 | async-start | bytes 1769472 | tf_op jit(solution)/shard_map/all_gather | solution.py:129
  724.4 71.8 %reduce-scatter.27.cloned.1.call-start = ((), (), s32[]{:S(2)}) async-start(), calls=%async_computation.25 | async-start | bytes 1769472 | tf_op jit(solution)/shard_map/reduce_scatter | solution.py:121
  774.2 46.2 %all-gather.26.cloned.1.call-start = ((), (), s32[]{:S(2)}) async-start(), calls=%async_computation.26 | async-start | bytes 1769472 | tf_op jit(solution)/shard_map/all_gather | solution.py:129
  796.3 72.0 %reduce-scatter.29.cloned.1.call-start = ((), (), s32[]{:S(2)}) async-start(), calls=%async_computation.27 | async-start | bytes 1769472 | tf_op jit(solution)/shard_map/reduce_scatter | solution.py:121
  846.3 46.3 %all-gather.28.cloned.1.call-start = ((), (), s32[]{:S(2)}) async-start(), calls=%async_computation.28 | async-start | bytes 1769472 | tf_op jit(solution)/shard_map/all_gather | solution.py:129
  906.9 72.2 %all-to-all-start.1 = ((bf16[16,48,1152]{2,1,0:T(8,128)(2,1)}), bf16[16,48,1152]{2,1,0:T(8,128)(2,1)S(1)}, u32[]{:S(2)}, u32[]{:S(2)}) async-start(bf16[16,48,1152]{2,1,0:T(8,128)(2,1)} %bitcast.183), calls=%async_computation.9 | async-start | bytes 3538944 | tf_op jit(solution)/shard_map/all_to_all | solution.py:398
  913.0 56.9 %reduce-scatter.33.cloned.1.call-start = ((), (), s32[]{:S(2)}) async-start(), calls=%async_computation.30 | async-start | bytes 208896
  (68 other events, 1123.3 us)
Sparse Core Ops, SparseCore 0:
  10.9 45.7 all-gather.11
  59.6 37.1 all-gather.13
  99.7 45.7 all-gather.15
  148.0 39.0 all-gather.17
  193.7 57.8 reduce-scatter.30
  255.1 57.2 reduce-scatter.16
  316.3 66.7 reduce-scatter.14
  386.9 67.1 reduce-scatter.18
  457.2 35.9 all-reduce.4
  549.8 21.9 reduce-scatter.20
  573.4 22.7 all-gather.19
  631.6 21.8 reduce-scatter.22
  655.0 22.7 all-gather.21
  702.5 21.8 reduce-scatter.24
  725.8 22.7 all-gather.23
  774.4 21.8 reduce-scatter.26
  797.6 22.7 all-gather.25
  846.4 21.8 reduce-scatter.28
  869.9 22.7 all-gather.27
  918.3 51.5 reduce-scatter.32
where the time goes:
time: 1010 us; the launch traced here: 999 us
  waiting for transfers between devices  650 us (64%)
  matrix products  158 us (16%)
  blocking collectives  117 us (12%)
  other arithmetic  26.2 us (3%)
  local copies, waits for them, and re-layouts  22.8 us (2%)
  between operations  16.3 us (2%)
    all_gather x5, waiting for transfers between devices, gram_of(): lax.all_gather(gram_share.astype(jnp.bfloat16), 'ctx', axis=0, tiled=True)  120 us
    reduce_scatter x5, waiting for transfers between devices, gram_of(): lax.psum_scatter(jnp.dot(picked, iterate.T, precision=highest, preferred_...  110 us
    reduce_scatter x1, waiting for transfers between devices, per_device(): lax.psum_scatter(grad_in.astype(jnp.bfloat16), 'dp', scatter_dimension=0,...  71.1 us
    reduce_scatter x1, waiting for transfers between devices, per_device(): lax.psum_scatter(grad_qkv.astype(jnp.bfloat16), 'dp', scatter_dimension=0...  70.7 us
    reduce_scatter x1, waiting for transfers between devices, per_device(): lax.psum_scatter(grad_out.astype(jnp.bfloat16), 'dp', scatter_dimension=0...  59 us
    unnamed x22, waiting for transfers between devices  56.3 us
    dot_general x5, matrix products, gram_of(): jnp.dot(picked, iterate.T, precision=highest, preferred_element_type=jnp....  46.8 us
    all_gather x1, waiting for transfers between devices, per_device(): lax.all_gather(w_in.astype(bf16), 'dp', axis=0, tiled=True)  46.7 us
  transfers between devices with their start and end apart: 21, of which 20 were waited for; matrix products, arithmetic and copies ran while one was open for 6% of the time, Pallas kernels for 0%

commit v1 on v0

--- a/solution.py
+++ b/solution.py
@@ -1,8 +1,11 @@
+import functools
 import math
 
 import jax
 import jax.numpy as jnp
 from jax import lax
+from jax.experimental import pallas as pl
+from jax.experimental.pallas import tpu as pltpu
 from jax.sharding import PartitionSpec as P
 
 HEADS = 12
@@ -437,6 +440,424 @@
     )
 
 
+def ring_places(mesh):
+    chip_count = mesh.shape["dp"] // 2
+    natural = list(range(chip_count))
+    try:
+        column = [mesh.devices[2 * chip, 0] for chip in natural]
+        partner = [mesh.devices[2 * chip + 1, 0] for chip in natural]
+        coords = [tuple(device.coords) for device in column]
+        if coords != [tuple(device.coords) for device in partner]:
+            return natural
+    except (AttributeError, IndexError):
+        return natural
+    dims = [dim for dim in range(3) if len({c[dim] for c in coords}) > 1]
+    narrow = [dim for dim in dims if len({c[dim] for c in coords}) == 2]
+    if len(dims) != 2 or not narrow:
+        return natural
+    split = narrow[0]
+    along = [dim for dim in dims if dim != split][0]
+    low = min(c[split] for c in coords)
+    first = sorted((c for c in natural if coords[c][split] == low), key=lambda c: coords[c][along])
+    second = sorted((c for c in natural if coords[c][split] != low), key=lambda c: -coords[c][along])
+    return first + second
+
+
+def place_rows(pieces, indices, widths):
+    count = len(pieces)
+    rows = pieces[0].shape[0]
+    offsets = [sum(widths[:k]) for k in range(len(widths))]
+
+    def body(*refs):
+        index_ref = refs[0]
+        piece_refs = refs[1 : 1 + count]
+        out_refs = refs[1 + count : 1 + count + len(widths)]
+        sems = refs[-1]
+        copies = []
+        for piece_at in range(count):
+            start = pl.multiple_of(index_ref[piece_at] * rows, rows)
+            for width_at, width in enumerate(widths):
+                source = piece_refs[piece_at].at[:, pl.ds(offsets[width_at], width)]
+                target = out_refs[width_at].at[pl.ds(start, rows), :]
+                copies.append(
+                    pltpu.make_async_copy(source, target, sems.at[piece_at, width_at])
+                )
+        for copy in copies:
+            copy.start()
+        for copy in copies:
+            copy.wait()
+
+    anywhere = pl.BlockSpec(memory_space=pl.ANY)
+    return pl.pallas_call(
+        body,
+        in_specs=[pl.BlockSpec(memory_space=pltpu.SMEM)] + [anywhere] * count,
+        out_specs=[anywhere] * len(widths),
+        out_shape=[
+            jax.ShapeDtypeStruct((count * rows, width), pieces[0].dtype) for width in widths
+        ],
+        scratch_shapes=[pltpu.SemaphoreType.DMA((count, len(widths)))],
+    )(indices, *pieces)
+
+
+def sweep_rows(start_rows, picked_rows):
+    high = lax.Precision.HIGH
+    f32 = jnp.float32
+    gram = contract_cols(start_rows, start_rows)
+    inverse = 1.0 / (jnp.sqrt(jnp.trace(gram)) + ortho_eps)
+    gram = gram * (inverse * inverse)
+    identity = jnp.eye(gram.shape[0], dtype=f32)
+    top = None
+    for sweep_index in range(NS_ITERS):
+        last = sweep_index + 1 == NS_ITERS
+        if last and top is not None:
+            inner = quintic_two * top + quintic_three * jnp.dot(top, gram, precision=high)
+            top = quintic_one * top + jnp.dot(inner, gram, precision=high)
+            break
+        square = jnp.dot(gram, gram, precision=high)
+        factor = quintic_one * identity + quintic_two * gram + quintic_three * square
+        if top is None:
+            top = factor[:picked_rows]
+        else:
+            top = jnp.dot(top, factor, precision=high)
+        if not last:
+            gram = jnp.dot(jnp.dot(gram, factor, precision=high), factor, precision=high)
+    return jnp.dot((top * inverse).astype(jnp.bfloat16), start_rows, preferred_element_type=f32)
+
+
+def paired_device(order, *arrays):
+    (
+        block_input,
+        out_grad,
+        positions,
+        w_qkv,
+        w_attn_out,
+        w_in,
+        w_mlp_out,
+        norm_gains,
+        m_qkv,
+        m_attn_out,
+        m_in,
+        m_mlp_out,
+        gain_mean,
+        gain_var,
+    ) = arrays
+    bf16 = jnp.bfloat16
+    f32 = jnp.float32
+    dp_count = lax.axis_size("dp")
+    ctx_count = lax.axis_size("ctx")
+    chip_count = dp_count // 2
+    dp_at = lax.axis_index("dp")
+    half_at = lax.axis_index("ctx")
+    low_half = half_at == 0
+    core_at = dp_at % 2
+    tok_rows = block_input.shape[1]
+    width = block_input.shape[2]
+    length = tok_rows * ctx_count
+    heads = HEADS // ctx_count
+    head_size = width // HEADS
+    span = heads * head_size
+    score_scale = 1.0 / math.sqrt(head_size)
+    owned_rows = w_qkv.shape[0]
+    hidden_units = w_mlp_out.shape[1]
+    hidden_half = hidden_units // 2
+    place = [0] * chip_count
+    for spot, chip in enumerate(order):
+        place[chip] = spot
+    order_table = jnp.array(order, jnp.int32)
+    spot_at = jnp.array(place, jnp.int32)[dp_at // 2]
+
+    def ring_pairs(step):
+        return [
+            (2 * order[spot] + core, 2 * order[(spot + step) % chip_count] + core)
+            for spot in range(chip_count)
+            for core in range(2)
+        ]
+
+    forward_pairs = ring_pairs(1)
+    backward_pairs = ring_pairs(-1)
+    core_pairs = [(index, index ^ 1) for index in range(dp_count)]
+    flip_pairs = [(0, 1), (1, 0)]
+
+    def chip_index(step):
+        return order_table[(spot_at + step + chip_count) % chip_count]
+
+    def swap_core(value):
+        return lax.ppermute(value, "dp", core_pairs)
+
+    def swap_half(value):
+        return lax.ppermute(value, "ctx", flip_pairs)
+
+    ahead_steps = chip_count // 2
+    behind_steps = chip_count - 1 - ahead_steps
+
+    def ring_collect(shard):
+        steps = [0]
+        pieces = [shard]
+        ahead = shard
+        behind = shard
+        for step in range(1, ahead_steps + 1):
+            ahead = lax.ppermute(ahead, "dp", forward_pairs)
+            steps.append(-step)
+            pieces.append(ahead)
+            if step <= behind_steps:
+                behind = lax.ppermute(behind, "dp", backward_pairs)
+                steps.append(step)
+                pieces.append(behind)
+        return steps, pieces
+
+    def collect(shard, widths):
+        steps, pieces = ring_collect(shard)
+        others = [swap_core(piece) for piece in pieces]
+        chips = jnp.stack([chip_index(step) for step in steps])
+        indices = jnp.concatenate([2 * chips + core_at, 2 * chips + 1 - core_at])
+        return place_rows(pieces + others, indices, widths)
+
+    def ring_reduce(partial):
+        columns = partial.shape[1]
+        split = partial.reshape(chip_count, 2, owned_rows, columns)
+        even, odd = split[:, 0], split[:, 1]
+        is_even = core_at == 0
+        kept = jnp.where(is_even, even, odd)
+        given = jnp.where(is_even, odd, even)
+        chunks = (kept.astype(f32) + swap_core(given).astype(f32)).astype(bf16)
+
+        def chunk(step):
+            return lax.dynamic_index_in_dim(chunks, chip_index(step), 0, keepdims=False)
+
+        ahead = chunk(ahead_steps)
+        behind = chunk(-behind_steps)
+        for step in range(ahead_steps, 0, -1):
+            ahead = lax.ppermute(ahead, "dp", forward_pairs)
+            if step > 1:
+                ahead = (ahead.astype(f32) + chunk(step - 1).astype(f32)).astype(bf16)
+            if step <= behind_steps:
+                behind = lax.ppermute(behind, "dp", backward_pairs)
+                if step > 1:
+                    behind = (behind.astype(f32) + chunk(1 - step).astype(f32)).astype(bf16)
+        return (chunk(0).astype(f32) + ahead.astype(f32) + behind.astype(f32)).astype(bf16)
+
+    def my_half(matrix, parts):
+        rows = matrix.shape[0]
+        split = matrix.reshape(rows, parts, 2, -1)
+        picked = jnp.where(low_half, split[:, :, 0], split[:, :, 1])
+        return picked.reshape(rows, -1)
+
+    def ordered(own, other, axis):
+        first = jnp.where(low_half, own, other)
+        second = jnp.where(low_half, other, own)
+        return jnp.concatenate([first, second], axis=axis)
+
+    gain_columns = jnp.pad(jnp.transpose(norm_gains), ((0, 0), (0, 128 - norm_gains.shape[0])))
+    first_shard = jnp.concatenate([my_half(w_qkv, 3), gain_columns], axis=1).astype(bf16)
+    pad_units = -hidden_half % 128
+    second_shard = jnp.concatenate(
+        [
+            w_attn_out,
+            my_half(w_in, 2),
+            jnp.pad(my_half(w_mlp_out, 1), ((0, 0), (0, pad_units))),
+        ],
+        axis=1,
+    ).astype(bf16)
+
+    own_places = positions[0]
+    digits = jnp.stack([own_places // 128, own_places % 128]).astype(bf16)
+    digit_rows = jnp.pad(digits, ((0, 14), (0, width - tok_rows)))
+    own_pack = jnp.concatenate([block_input[0], out_grad[0], digit_rows], axis=0)
+    other_pack = swap_half(own_pack)
+    w_qkv_h, gains_t = collect(first_shard, (3 * span, 128))
+    w_out_b, w_in_h, w_mlp_p = collect(
+        second_shard, (width, 2 * hidden_half, hidden_half + pad_units)
+    )
+    w_mlp_h = w_mlp_p[:, :hidden_half]
+
+    other_digits = other_pack[2 * tok_rows : 2 * tok_rows + 2, :tok_rows].astype(jnp.int32)
+    other_places = other_digits[0] * 128 + other_digits[1]
+    places = ordered(own_places, other_places, 0)
+    x_wide = ordered(own_pack[:tok_rows], other_pack[:tok_rows], 0).astype(f32)
+    dy_b = ordered(own_pack[tok_rows : 2 * tok_rows], other_pack[tok_rows : 2 * tok_rows], 0)
+    cosine, sine = rope_tables(places, head_size)
+    starts = jnp.arange(length, dtype=jnp.int32) - places
+    same = (starts[:, None] == starts[None, :])[None]
+    gains_w = gains_t[:, :2].astype(f32)
+    gain_one = gains_w[:, 0]
+    gain_two = gains_w[:, 1]
+
+    hat_one, factor_one = normalize(x_wide)
+    act_one = (hat_one * gain_one).astype(bf16)
+    qkv = jnp.dot(act_one, w_qkv_h, preferred_element_type=f32)
+    queries_b = rotate(qkv[:, :span].reshape(length, heads, head_size), cosine, sine).astype(bf16)
+    keys_b = rotate(qkv[:, span : 2 * span].reshape(length, heads, head_size), cosine, sine).astype(
+        bf16
+    )
+    values_b = qkv[:, 2 * span :].astype(bf16).reshape(length, heads, head_size)
+    scores = (
+        jnp.einsum("qhd,khd->hqk", queries_b, keys_b, preferred_element_type=f32) * score_scale
+    )
+    weights = jnp.where(same, jnp.exp(scores), 0.0)
+    totals = jnp.sum(weights, axis=-1)
+    summed = jnp.einsum("hqk,khd->qhd", weights.astype(bf16), values_b, preferred_element_type=f32)
+    attended = summed / jnp.transpose(totals)[:, :, None]
+    log_total = jnp.log(totals)
+    own_mixed = attended.reshape(length, span).astype(bf16)
+    mixed_b = ordered(own_mixed, swap_half(own_mixed), 1)
+
+    hidden = x_wide + jnp.dot(mixed_b, w_out_b, preferred_element_type=f32)
+    hat_two, factor_two = normalize(hidden)
+    act_two = (hat_two * gain_two).astype(bf16)
+    lifted = jnp.dot(act_two, w_in_h, preferred_element_type=f32)
+    preact = lifted[:, :hidden_half]
+    gate_half = lifted[:, hidden_half:]
+    activated, derivative = gelu_parts(preact)
+    inner_b = (activated * gate_half).astype(bf16)
+    grad_inner = jnp.dot(dy_b, w_mlp_h, preferred_element_type=f32)
+    grad_lift = jnp.concatenate(
+        [grad_inner * gate_half * derivative, grad_inner * activated], axis=1
+    ).astype(bf16)
+    grad_two_part = contract_cols(grad_lift, w_in_h)
+    grad_act_two = grad_two_part + swap_half(grad_two_part.astype(bf16)).astype(f32)
+
+    def own_tokens(field):
+        return jnp.where(low_half, field[:tok_rows], field[tok_rows:])
+
+    def other_tokens(field):
+        return jnp.where(low_half, field[tok_rows:], field[:tok_rows])
+
+    out_part = contract_cols(inner_b, w_mlp_h)
+    output = (
+        own_tokens(hidden)
+        + own_tokens(out_part)
+        + swap_half(other_tokens(out_part).astype(bf16)).astype(f32)
+    )
+    grad_mlp = contract_rows(dy_b, inner_b)
+    grad_in = contract_rows(act_two, grad_lift)
+    early_rows = ring_reduce(jnp.concatenate([grad_in, grad_mlp], axis=1).astype(bf16))
+
+    gain_grad_two = jnp.sum(grad_two_part * hat_two, axis=0)
+    grad_hidden = dy_b.astype(f32) + normalize_back(grad_act_two * gain_two, hat_two, factor_two)
+    grad_hidden_b = grad_hidden.astype(bf16)
+    grad_out = contract_rows(
+        mixed_b, jnp.where(low_half, grad_hidden_b[:, :span], grad_hidden_b[:, span:])
+    )
+    out_rows_h = jnp.where(low_half, w_out_b[:span], w_out_b[span:])
+    grad_mixed = contract_cols(grad_hidden_b, out_rows_h).reshape(length, heads, head_size)
+    delta = jnp.sum(grad_mixed * attended, axis=-1)
+    grad_mixed_b = grad_mixed.astype(bf16)
+    probs = jnp.where(same, jnp.exp(scores - log_total[:, :, None]), 0.0)
+    grad_probs = jnp.einsum("qhd,khd->hqk", grad_mixed_b, values_b, preferred_element_type=f32)
+    grad_scores_b = (probs * (grad_probs - jnp.transpose(delta)[:, :, None])).astype(bf16)
+    query_grad = (
+        jnp.einsum("hqk,khd->qhd", grad_scores_b, keys_b, preferred_element_type=f32) * score_scale
+    )
+    key_grad = (
+        jnp.einsum("hqk,qhd->khd", grad_scores_b, queries_b, preferred_element_type=f32)
+        * score_scale
+    )
+    value_grad = jnp.einsum(
+        "hqk,qhd->khd", probs.astype(bf16), grad_mixed_b, preferred_element_type=f32
+    )
+    grad_qkv_in = jnp.concatenate(
+        [
+            rotate_back(query_grad, cosine, sine).reshape(length, span),
+            rotate_back(key_grad, cosine, sine).reshape(length, span),
+            value_grad.reshape(length, span),
+        ],
+        axis=1,
+    ).astype(bf16)
+    grad_qkv = contract_rows(act_one, grad_qkv_in)
+    grad_one_part = contract_cols(grad_qkv_in, w_qkv_h)
+    gain_grad_one = jnp.sum(grad_one_part * hat_one, axis=0)
+    gain_pair = jnp.pad(jnp.stack([gain_grad_one, gain_grad_two], axis=1), ((0, 0), (0, 126)))
+    late_rows = ring_reduce(jnp.concatenate([grad_qkv, grad_out, gain_pair], axis=1).astype(bf16))
+
+    grad_act_one = own_tokens(grad_one_part) + swap_half(
+        other_tokens(grad_one_part).astype(bf16)
+    ).astype(f32)
+    grad_input = own_tokens(grad_hidden) + normalize_back(
+        grad_act_one * gain_one, own_tokens(hat_one), own_tokens(factor_one)
+    )
+
+    def whole_columns(own, other, parts):
+        rows = own.shape[0]
+        first = jnp.where(low_half, own, other).reshape(rows, parts, -1)
+        second = jnp.where(low_half, other, own).reshape(rows, parts, -1)
+        return jnp.stack([first, second], axis=2).reshape(rows, -1).astype(f32)
+
+    factor = 1.0 / math.sqrt(dp_count * length)
+    early_other = swap_half(early_rows)
+    late_other = swap_half(late_rows)
+    cut = 2 * hidden_half
+    grads = [
+        whole_columns(late_rows[:, : 3 * span], late_other[:, : 3 * span], 3) * factor,
+        whole_columns(
+            late_rows[:, 3 * span : 3 * span + span], late_other[:, 3 * span : 3 * span + span], 1
+        )
+        * factor,
+        whole_columns(early_rows[:, :cut], early_other[:, :cut], 2) * factor,
+        whole_columns(early_rows[:, cut:], early_other[:, cut:], 1) * factor,
+    ]
+    gain_sum = late_rows[:, 4 * span :].astype(f32) + late_other[:, 4 * span :].astype(f32)
+    gain_grad = jnp.transpose(gain_sum)[:2] * factor
+
+    matrices = (w_qkv, w_attn_out, w_in, w_mlp_out)
+    moments = (m_qkv, m_attn_out, m_in, m_mlp_out)
+    moments_next = [momentum_rate * moment + grad for moment, grad in zip(moments, grads)]
+    widest = max(moment.shape[1] for moment in moments)
+    slots = jnp.stack(
+        [
+            jnp.pad(moment.astype(bf16), ((0, 0), (0, widest - moment.shape[1])))
+            for moment in moments_next
+        ]
+    )
+    group = dp_count // 4
+    group_at = dp_at // group
+
+    def shift_pairs(step):
+        return [(index, (index + step * group) % dp_count) for index in range(dp_count)]
+
+    blocks = [lax.dynamic_index_in_dim(slots, group_at, 0, keepdims=False)]
+    for step in range(1, 4):
+        given = lax.dynamic_index_in_dim(slots, (group_at + step) % 4, 0, keepdims=False)
+        blocks.append(lax.ppermute(given, "dp", shift_pairs(step)))
+    held = jnp.concatenate(blocks, axis=0)
+    reach = 2
+    while reach < group:
+        pairs = [(index, index ^ reach) for index in range(dp_count)]
+        held = jnp.concatenate([held, lax.ppermute(held, "dp", pairs)], axis=0)
+        reach *= 2
+    held = jnp.concatenate([held, swap_core(held)], axis=0)
+    turned = sweep_rows(held, 4 * owned_rows).astype(bf16).reshape(4, owned_rows, widest)
+    returned = [turned[0]]
+    for step in range(1, 4):
+        returned.append(lax.ppermute(turned[step], "dp", shift_pairs(-step)))
+    updates = jnp.stack(returned)
+    new_weights = []
+    for slot_index, weight in enumerate(matrices):
+        update = lax.dynamic_index_in_dim(updates, (slot_index - group_at + 4) % 4, 0, False)
+        rate = matrix_rate * math.sqrt(max(weight.shape[0] * dp_count, weight.shape[1]))
+        new_weights.append(weight - rate * update[:, : weight.shape[1]].astype(f32))
+    mean_next = beta_first * gain_mean + (1.0 - beta_first) * gain_grad
+    var_next = beta_second * gain_var + (1.0 - beta_second) * gain_grad * gain_grad
+    gains_next = norm_gains - gain_rate * (mean_next / first_fix) / (
+        jnp.sqrt(var_next / second_fix) + adam_eps
+    )
+    return (
+        output.astype(bf16)[None],
+        grad_input[None],
+        *grads,
+        gain_grad,
+        *new_weights,
+        gains_next,
+        *moments_next,
+        mean_next,
+        var_next,
+    )
+
+
+def fits_pairs(mesh):
+    dp_count, ctx_count = mesh.shape["dp"], mesh.shape["ctx"]
+    return ctx_count == 2 and HEADS % 2 == 0 and dp_count % 8 == 0
+
+
 def solution(mesh):
     placed = (
         P("dp", "ctx", None),
@@ -454,8 +875,11 @@
         P(None, "dp"),
         P(None, "dp"),
     )
+    body = per_device
+    if fits_pairs(mesh):
+        body = functools.partial(paired_device, ring_places(mesh))
     return jax.shard_map(
-        per_device,
+        body,
         mesh=mesh,
         in_specs=placed,
         out_specs=(

time: 1010 us -> 564 us (0.56)
  waiting for transfers between devices: 650 us -> 123 us
  Pallas kernels: 0 us -> 183 us
  blocking collectives: 117 us -> 0 us
  matrix products: 158 us -> 74.3 us
  starting transfers between devices: 7.94 us -> 48.5 us
  local copies, waits for them, and re-layouts: 22.8 us -> 58.9 us
  other arithmetic: 26.2 us -> 43.5 us
    reduce_scatter x8 -> x0, waiting for transfers between devices: 311 us -> none  [the longest x5 110 us: gram_of(): lax.psum_scatter(jnp.dot(picked, iterate.T, precision=highest, preferred_...]
    all_gather x9 -> x0, waiting for transfers between devices: 245 us -> none  [the longest x5 120 us: gram_of(): lax.all_gather(gram_share.astype(jnp.bfloat16), 'ctx', axis=0, tiled=True)]
    pallas_call x0 -> x2, Pallas kernels: none -> 183 us  [place_rows(): pl.pallas_call(body, in_specs=[pl.BlockSpec(memory_space=pltpu.SMEM)] + [...]
    ppermute x0 -> x61, waiting for transfers between devices: none -> 123 us  [the longest x8 44.4 us: ring_reduce(): ahead = lax.ppermute(ahead, 'dp', forward_pairs)]
    dot_general x25 -> x28, matrix products: 138 us -> 58.2 us  [the longest x4 16.6 us: sweep_rows(): square = jnp.dot(gram, gram, precision=high)]
    all_gather x9 -> x0, blocking collectives: 67.2 us -> none  [the longest x1 16.7 us: per_device(): lax.all_gather(norm_gains.astype(bf16), 'dp', axis=1, tiled=True)]
    unnamed x22 -> x0, waiting for transfers between devices: 56.3 us -> none
    ppermute x0 -> x61, starting transfers between devices: none -> 48.5 us  [the longest x6 8.26 us: ring_collect(): behind = lax.ppermute(behind, 'dp', backward_pairs)]
  transfers between devices with their start and end apart: 21 -> 61, of which waited for: 20 -> 22; matrix products, arithmetic and copies ran while one was open for 6% -> 18% of each run, Pallas kernels for 0% -> 11%
where the time goes in v1:
time: 564 us; the launch traced here: 556 us
  Pallas kernels  183 us (32%)
  waiting for transfers between devices  123 us (22%)
  matrix products  74.3 us (13%)
  local copies, waits for them, and re-layouts  58.9 us (10%)
  starting transfers between devices  48.5 us (9%)
  other arithmetic  43.5 us (8%)
  between operations  25.1 us (4%)
    pallas_call x2, Pallas kernels, place_rows(): pl.pallas_call(body, in_specs=[pl.BlockSpec(memory_space=pltpu.SMEM)] + [...  183 us
    ppermute x8, waiting for transfers between devices, ring_reduce(): ahead = lax.ppermute(ahead, 'dp', forward_pairs)  44.4 us
    unnamed x230, local copies, waits for them, and re-layouts  21 us
    ppermute x1, waiting for transfers between devices, paired_device(): held = jnp.concatenate([held, lax.ppermute(held, 'dp', pairs)], axis=0)  18.7 us
    dot_general x4, matrix products, sweep_rows(): square = jnp.dot(gram, gram, precision=high)  16.6 us
    ppermute x7, waiting for transfers between devices, swap_half(): return lax.ppermute(value, 'ctx', flip_pairs)  16.2 us
    ppermute x3, waiting for transfers between devices, paired_device(): returned.append(lax.ppermute(turned[step], 'dp', shift_pairs(-step)))  16.1 us
    ppermute x3, waiting for transfers between devices, paired_device(): blocks.append(lax.ppermute(given, 'dp', shift_pairs(step)))  13.8 us
  transfers between devices with their start and end apart: 61, of which 22 were waited for; matrix products, arithmetic and copies ran while one was open for 18% of the time, Pallas kernels for 11%

profile of v1, /device:TPU:26, one launch (start us, length us, event | category | flops | bytes accessed | tf_op | source)
XLA Modules:
  0.0 556.5 jit_solution(12362165437430589834)
XLA Ops:
  17.9 5.2 stack.62
  37.3 5.5 collective-permute-done.7.refs_8_
  46.6 61.6 %shard_map.295 = (bf16[768,1152]{1,0:T(8,128)(2,1)}, bf16[768,128]{1,0:T(8,128)(2,1)}) custom-call(s32[16]{0:T(128)} %pad_add_fusion.1.refs_0_, bf16[48,1280]{1,0:T(8,128)(2,1)} %copy-done.44, bf16[48,1280]{1,0:T(8,128)(2,1)} %copy-done.77, bf16[48,1280]{1,0:T(8,128)(2,1)} %copy-done.78, bf16[48,1280]{1,0:T(8,128)(2,1)} %copy-done.80, ...), custom_call_target="tpu_custom_call" | custom-call | tf_op jit(solution)/shard_map/pallas_call | solution.py:491
  136.1 121.3 %shard_map.296 = (bf16[768,768]{1,0:T(8,128)(2,1)}, bf16[768,1152]{1,0:T(8,128)(2,1)}, bf16[768,640]{1,0:T(8,128)(2,1)}) custom-call(s32[16]{0:T(128)} %pad_add_fusion.1.refs_0_, bf16[48,2560]{1,0:T(8,128)(2,1)} %copy-done.32, bf16[48,2560]{1,0:T(8,128)(2,1)} %copy-done.61, bf16[48,2560]{1,0:T(8,128)(2,1)} %copy-done.62, bf16[48,2560]{1,0:T(8,128)(2,1)} %copy-done.63, ...), custom_call_target="tpu_custom_call" | custom-call | tf_op jit(solution)/shard_map/pallas_call | solution.py:491
  274.0 4.5 copy.326
  305.3 4.5 copy.325
  322.7 4.5 copy.300
  327.2 4.5 fusion
  336.2 8.0 %collective-permute-done.45 = bf16[48,1728]{0,1:T(8,128)(2,1)S(1)} collective-permute-done((bf16[48,1728]{0,1:T(8,128)(2,1)S(1)}, bf16[48,1728]{0,1:T(8,128)(2,1)S(1)}, u32[]{:S(2)}, u32[]{:S(2)}) %collective-permute-start.45) | collective-permute-done | bytes 165920 | tf_op jit(solution)/shard_map/ppermute | solution.py:630
  345.7 4.9 copy.287
  350.5 4.5 fusion.1
  361.1 6.7 %collective-permute-done.36 = bf16[48,1664]{0,1:T(8,128)(2,1)S(1)} collective-permute-done((bf16[48,1664]{0,1:T(8,128)(2,1)S(1)}, bf16[48,1664]{0,1:T(8,128)(2,1)S(1)}, u32[]{:S(2)}, u32[]{:S(2)}) %collective-permute-start.36) | collective-permute-done | bytes 159776 | tf_op jit(solution)/shard_map/ppermute | solution.py:630
  368.6 8.7 %collective-permute-done.47 = bf16[48,1728]{0,1:T(8,128)(2,1)S(1)} collective-permute-done((bf16[48,1728]{0,1:T(8,128)(2,1)S(1)}, bf16[48,1728]{0,1:T(8,128)(2,1)S(1)}, u32[]{:S(2)}, u32[]{:S(2)}) %collective-permute-start.47) | collective-permute-done | bytes 165920 | tf_op jit(solution)/shard_map/ppermute | solution.py:630
  379.6 6.8 %collective-permute-done.37 = bf16[48,1664]{0,1:T(8,128)(2,1)S(1)} collective-permute-done((bf16[48,1664]{0,1:T(8,128)(2,1)S(1)}, bf16[48,1664]{0,1:T(8,128)(2,1)S(1)}, u32[]{:S(2)}, u32[]{:S(2)}) %collective-permute-start.37) | collective-permute-done | bytes 159776 | tf_op jit(solution)/shard_map/ppermute | solution.py:630
  388.7 7.2 %collective-permute-done.48 = bf16[48,1728]{0,1:T(8,128)(2,1)S(1)} collective-permute-done((bf16[48,1728]{0,1:T(8,128)(2,1)S(1)}, bf16[48,1728]{0,1:T(8,128)(2,1)S(1)}, u32[]{:S(2)}, u32[]{:S(2)}) %collective-permute-start.48) | collective-permute-done | bytes 165920 | tf_op jit(solution)/shard_map/ppermute | solution.py:630
  396.7 5.6 %collective-permute-done.38 = bf16[48,1664]{0,1:T(8,128)(2,1)S(1)} collective-permute-done((bf16[48,1664]{0,1:T(8,128)(2,1)S(1)}, bf16[48,1664]{0,1:T(8,128)(2,1)S(1)}, u32[]{:S(2)}, u32[]{:S(2)}) %collective-permute-start.38) | collective-permute-done | bytes 159776 | tf_op jit(solution)/shard_map/ppermute | solution.py:630
  414.2 7.6 %collective-permute-done.43 = bf16[48,1664]{0,1:T(8,128)(2,1)S(1)} collective-permute-done((bf16[48,1664]{0,1:T(8,128)(2,1)S(1)}, bf16[48,1664]{0,1:T(8,128)(2,1)S(1)}, u32[]{:S(2)}, u32[]{:S(2)}) %collective-permute-start.43) | collective-permute-done | bytes 159776 | tf_op jit(solution)/shard_map/ppermute | solution.py:588
  428.7 5.7 %collective-permute-done.53 = bf16[48,2304]{1,0:T(8,128)(2,1)S(1)} collective-permute-done((bf16[48,2304]{1,0:T(8,128)(2,1)S(1)}, bf16[48,2304]{1,0:T(8,128)(2,1)S(1)}, u32[]{:S(2)}, u32[]{:S(2)}) %collective-permute-start.53) | collective-permute-done | bytes 221216 | tf_op jit(solution)/shard_map/ppermute | solution.py:820
  434.4 8.1 %collective-permute-done.54 = bf16[48,2304]{1,0:T(8,128)(2,1)S(1)} collective-permute-done((bf16[48,2304]{1,0:T(8,128)(2,1)S(1)}, bf16[48,2304]{1,0:T(8,128)(2,1)S(1)}, u32[]{:S(2)}, u32[]{:S(2)}) %collective-permute-start.54) | collective-permute-done | bytes 221216 | tf_op jit(solution)/shard_map/ppermute | solution.py:820
  442.8 18.7 %collective-permute-done.56 = bf16[192,2304]{1,0:T(8,128)(2,1)S(1)} collective-permute-done((bf16[192,2304]{1,0:T(8,128)(2,1)S(1)}, bf16[192,2304]{1,0:T(8,128)(2,1)S(1)}, u32[]{:S(2)}, u32[]{:S(2)}) %collective-permute-start.56) | collective-permute-done | bytes 884768 | tf_op jit(solution)/shard_map/ppermute | solution.py:825
  464.0 5.6 %collective-permute-done.32 = bf16[128,768]{1,0:T(8,128)(2,1)S(1)} collective-permute-done((bf16[128,768]{1,0:T(8,128)(2,1)S(1)}, bf16[128,768]{1,0:T(8,128)(2,1)S(1)}, u32[]{:S(2)}, u32[]{:S(2)}) %collective-permute-start.32) | collective-permute-done | bytes 196640 | tf_op jit(solution)/shard_map/ppermute | solution.py:588
  476.0 5.0 select_reduce_fusion
  481.7 6.5 %fusion.2 = f32[768,768]{1,0:T(8,128)S(1)} fusion(f32[768,768]{1,0:T(8,128)} %get-tuple-element.211, f32[]{:T(128)S(6)} %mul.587), kind=kOutput, calls=%fused_computation.16 | convolution fusion | flops 2722627584 | bytes 4718596 | tf_op jit(solution)/shard_map/dot_general | solution.py:516
  538.3 15.3 %collective-permute-done.59 = bf16[48,2304]{1,0:T(8,128)(2,1)S(1)} collective-permute-done((bf16[48,2304]{1,0:T(8,128)(2,1)S(1)}, bf16[48,2304]{1,0:T(8,128)(2,1)S(1)}, u32[]{:S(2)}, u32[]{:S(2)}) %collective-permute-start.59) | collective-permute-done | bytes 221216 | tf_op jit(solution)/shard_map/ppermute | solution.py:831
  (498 shorter events, 194.9 us)
Async XLA Ops:
  4.1 22.5 %collective-permute-start.17 = (bf16[48,2560]{1,0:T(8,128)(2,1)S(1)}, bf16[48,2560]{1,0:T(8,128)(2,1)S(1)}, u32[]{:S(2)}, u32[]{:S(2)}) collective-permute-start(bf16[48,2560]{1,0:T(8,128)(2,1)S(1)} %fusion.126.refs_1_), channel_id=1, source_target_pairs={{0,8},{2,10},{8,16},{10,18},{16,24},{18,26},{24,28},{26,30},{28,20... | collective-permute-start | bytes 737288 | tf_op jit(solution)/shard_map/ppermute | solution.py:599
  4.6 26.9 %collective-permute-start.18 = (bf16[48,2560]{1,0:T(8,128)(2,1)S(1)}, bf16[48,2560]{1,0:T(8,128)(2,1)S(1)}, u32[]{:S(2)}, u32[]{:S(2)}) collective-permute-start(bf16[48,2560]{1,0:T(8,128)(2,1)S(1)} %fusion.126.refs_1_), channel_id=1, source_target_pairs={{0,4},{2,6},{8,0},{10,2},{16,8},{18,10},{24,16},{26,18},{28,24},{3... | collective-permute-start | bytes 737288 | tf_op jit(solution)/shard_map/ppermute | solution.py:603
  6.9 16.9 %collective-permute-start.1 = (bf16[48,1280]{1,0:T(8,128)(2,1)S(1)}, bf16[48,1280]{1,0:T(8,128)(2,1)S(1)}, u32[]{:S(2)}, u32[]{:S(2)}) collective-permute-start(bf16[48,1280]{1,0:T(8,128)(2,1)S(1)} %fusion.135.refs_1_), channel_id=1, source_target_pairs={{0,8},{2,10},{8,16},{10,18},{16,24},{18,26},{24,28},{26,30},{28,20... | collective-permute-start | bytes 368648 | tf_op jit(solution)/shard_map/ppermute | solution.py:599
  7.4 16.4 %collective-permute-start.2 = (bf16[48,1280]{1,0:T(8,128)(2,1)S(1)}, bf16[48,1280]{1,0:T(8,128)(2,1)S(1)}, u32[]{:S(2)}, u32[]{:S(2)}) collective-permute-start(bf16[48,1280]{1,0:T(8,128)(2,1)S(1)} %fusion.135.refs_1_), channel_id=1, source_target_pairs={{0,4},{2,6},{8,0},{10,2},{16,8},{18,10},{24,16},{26,18},{28,24},{3... | collective-permute-start | bytes 368648 | tf_op jit(solution)/shard_map/ppermute | solution.py:603
  42.8 73.1 %collective-permute-start.24 = (bf16[48,2560]{1,0:T(8,128)(2,1)S(1)}, bf16[48,2560]{1,0:T(8,128)(2,1)}, u32[]{:S(2)}, u32[]{:S(2)}) collective-permute-start(bf16[48,2560]{1,0:T(8,128)(2,1)S(1)} %fusion.126.refs_1_), channel_id=1, source_target_pairs={{0,2},{2,0},{4,6},{6,4},{8,10},{10,8},{12,14},{14,12},{16,18},{18,... | collective-permute-start | bytes 737288 | tf_op jit(solution)/shard_map/ppermute | solution.py:585
  43.3 88.6 %collective-permute-start.25 = (bf16[48,2560]{1,0:T(8,128)(2,1)S(1)}, bf16[48,2560]{1,0:T(8,128)(2,1)}, u32[]{:S(2)}, u32[]{:S(2)}) collective-permute-start(bf16[48,2560]{1,0:T(8,128)(2,1)S(1)} %collective-permute-done.17.refs_2_), channel_id=1, source_target_pairs={{0,2},{2,0},{4,6},{6,4},{8,10},{10,8},{12,14},{14,12},{16,18},{18,... | collective-permute-start | bytes 737288 | tf_op jit(solution)/shard_map/ppermute | solution.py:585
  43.4 88.6 %collective-permute-start.26 = (bf16[48,2560]{1,0:T(8,128)(2,1)S(1)}, bf16[48,2560]{1,0:T(8,128)(2,1)}, u32[]{:S(2)}, u32[]{:S(2)}) collective-permute-start(bf16[48,2560]{1,0:T(8,128)(2,1)S(1)} %collective-permute-done.18.refs_3_), channel_id=1, source_target_pairs={{0,2},{2,0},{4,6},{6,4},{8,10},{10,8},{12,14},{14,12},{16,18},{18,... | collective-permute-start | bytes 737288 | tf_op jit(solution)/shard_map/ppermute | solution.py:585
  43.9 69.5 %collective-permute-start.21 = (bf16[48,2560]{1,0:T(8,128)(2,1)S(1)}, bf16[48,2560]{1,0:T(8,128)(2,1)}, u32[]{:S(2)}, u32[]{:S(2)}) collective-permute-start(bf16[48,2560]{1,0:T(8,128)(2,1)S(1)} %collective-permute-done.19.refs_4_), channel_id=1, source_target_pairs={{0,8},{2,10},{8,16},{10,18},{16,24},{18,26},{24,28},{26,30},{28,20... | collective-permute-start | bytes 737288 | tf_op jit(solution)/shard_map/ppermute | solution.py:599
  45.2 87.4 %collective-permute-start.22 = (bf16[48,2560]{1,0:T(8,128)(2,1)S(1)}, bf16[48,2560]{1,0:T(8,128)(2,1)}, u32[]{:S(2)}, u32[]{:S(2)}) collective-permute-start(bf16[48,2560]{1,0:T(8,128)(2,1)S(1)} %collective-permute-done.20.refs_5_), channel_id=1, source_target_pairs={{0,4},{2,6},{8,0},{10,2},{16,8},{18,10},{24,16},{26,18},{28,24},{3... | collective-permute-start | bytes 737288 | tf_op jit(solution)/shard_map/ppermute | solution.py:603
  113.3 19.7 %collective-permute-start.23 = (bf16[48,2560]{1,0:T(8,128)(2,1)}, bf16[48,2560]{1,0:T(8,128)(2,1)S(1)}, u32[]{:S(2)}, u32[]{:S(2)}) collective-permute-start(bf16[48,2560]{1,0:T(8,128)(2,1)} %collective-permute-done.21.refs_6_), channel_id=1, source_target_pairs={{0,8},{2,10},{8,16},{10,18},{16,24},{18,26},{24,28},{26,30},{28,20... | collective-permute-start | bytes 737288 | tf_op jit(solution)/shard_map/ppermute | solution.py:599
  115.9 16.8 %collective-permute-start.16 = (bf16[256,384]{1,0:T(8,128)(2,1)S(1)}, bf16[256,384]{1,0:T(8,128)(2,1)S(1)}, u32[]{:S(2)}, u32[]{:S(2)}) collective-permute-start(bf16[256,384]{1,0:T(8,128)(2,1)S(1)} %copy.270), channel_id=1, source_target_pairs={{0,1},{1,0},{2,3},{3,2},{4,5},{5,4},{6,7},{7,6},{8,9},{9,8},{10,11... | collective-permute-start | bytes 589832 | tf_op jit(solution)/shard_map/ppermute | solution.py:588
  264.2 23.0 %collective-permute-start.33 = (bf16[256,768]{1,0:T(8,128)(2,1)}, bf16[256,768]{1,0:T(8,128)(2,1)}, u32[]{:S(2)}, u32[]{:S(2)}) collective-permute-start(bf16[256,768]{1,0:T(8,128)(2,1)} %get-tuple-element.207), channel_id=1, source_target_pairs={{0,1},{1,0},{2,3},{3,2},{4,5},{5,4},{6,7},{7,6},{8,9},{9,8},{10,11... | collective-permute-start | bytes 1179656 | tf_op jit(solution)/shard_map/ppermute | solution.py:588
  285.0 37.7 %collective-permute-start.44 = (bf16[8,48,1728]{2,1,0:T(8,128)(2,1)}, bf16[8,48,1728]{2,1,0:T(8,128)(2,1)}, u32[]{:S(2)}, u32[]{:S(2)}) collective-permute-start(bf16[8,48,1728]{2,1,0:T(8,128)(2,1)} %copy.299), channel_id=1, source_target_pairs={{0,2},{2,0},{4,6},{6,4},{8,10},{10,8},{12,14},{14,12},{16,18},{18,... | collective-permute-start | bytes 3981320 | tf_op jit(solution)/shard_map/ppermute | solution.py:585
  322.7 23.0 %collective-permute-start.35 = (bf16[8,48,1664]{2,1,0:T(8,128)(2,1)}, bf16[8,48,1664]{2,1,0:T(8,128)(2,1)}, u32[]{:S(2)}, u32[]{:S(2)}) collective-permute-start(bf16[8,48,1664]{2,1,0:T(8,128)(2,1)} %copy.286), channel_id=1, source_target_pairs={{0,2},{2,0},{4,6},{6,4},{8,10},{10,8},{12,14},{14,12},{16,18},{18,... | collective-permute-start | bytes 3833864 | tf_op jit(solution)/shard_map/ppermute | solution.py:585
  334.7 21.0 %collective-permute-start.49 = (bf16[48,1728]{0,1:T(8,128)(2,1)}, bf16[48,1728]{0,1:T(8,128)(2,1)}, u32[]{:S(2)}, u32[]{:S(2)}) collective-permute-start(bf16[48,1728]{0,1:T(8,128)(2,1)} %get-tuple-element.111), channel_id=1, source_target_pairs={{0,4},{2,6},{8,0},{10,2},{16,8},{18,10},{24,16},{26,18},{28,24},{3... | collective-permute-start | bytes 497672 | tf_op jit(solution)/shard_map/ppermute | solution.py:634
  358.1 19.3 %collective-permute-start.47 = (bf16[48,1728]{0,1:T(8,128)(2,1)S(1)}, bf16[48,1728]{0,1:T(8,128)(2,1)S(1)}, u32[]{:S(2)}, u32[]{:S(2)}) collective-permute-start(bf16[48,1728]{0,1:T(8,128)(2,1)S(1)} %get-tuple-element.108), channel_id=1, source_target_pairs={{0,8},{2,10},{8,16},{10,18},{16,24},{18,26},{24,28},{26,30},{28,20... | collective-permute-start | bytes 497672 | tf_op jit(solution)/shard_map/ppermute | solution.py:630
  358.9 18.4 %collective-permute-start.50 = (bf16[48,1728]{0,1:T(8,128)(2,1)S(1)}, bf16[48,1728]{0,1:T(8,128)(2,1)S(1)}, u32[]{:S(2)}, u32[]{:S(2)}) collective-permute-start(bf16[48,1728]{0,1:T(8,128)(2,1)S(1)} %get-tuple-element.109), channel_id=1, source_target_pairs={{0,4},{2,6},{8,0},{10,2},{16,8},{18,10},{24,16},{26,18},{28,24},{3... | collective-permute-start | bytes 497672 | tf_op jit(solution)/shard_map/ppermute | solution.py:634
  360.1 19.5 %collective-permute-start.40 = (bf16[48,1664]{0,1:T(8,128)(2,1)S(1)}, bf16[48,1664]{0,1:T(8,128)(2,1)S(1)}, u32[]{:S(2)}, u32[]{:S(2)}) collective-permute-start(bf16[48,1664]{0,1:T(8,128)(2,1)S(1)} %get-tuple-element.117), channel_id=1, source_target_pairs={{0,4},{2,6},{8,0},{10,2},{16,8},{18,10},{24,16},{26,18},{28,24},{3... | collective-permute-start | bytes 479240 | tf_op jit(solution)/shard_map/ppermute | solution.py:634
  367.9 18.5 %collective-permute-start.37 = (bf16[48,1664]{0,1:T(8,128)(2,1)S(1)}, bf16[48,1664]{0,1:T(8,128)(2,1)S(1)}, u32[]{:S(2)}, u32[]{:S(2)}) collective-permute-start(bf16[48,1664]{0,1:T(8,128)(2,1)S(1)} %fusion.95), channel_id=1, source_target_pairs={{0,8},{2,10},{8,16},{10,18},{16,24},{18,26},{24,28},{26,30},{28,20... | collective-permute-start | bytes 479240 | tf_op jit(solution)/shard_map/ppermute | solution.py:630
  379.0 16.9 %collective-permute-start.48 = (bf16[48,1728]{0,1:T(8,128)(2,1)S(1)}, bf16[48,1728]{0,1:T(8,128)(2,1)S(1)}, u32[]{:S(2)}, u32[]{:S(2)}) collective-permute-start(bf16[48,1728]{0,1:T(8,128)(2,1)S(1)} %get-tuple-element.106), channel_id=1, source_target_pairs={{0,8},{2,10},{8,16},{10,18},{16,24},{18,26},{24,28},{26,30},{28,20... | collective-permute-start | bytes 497672 | tf_op jit(solution)/shard_map/ppermute | solution.py:630
  426.4 16.1 %collective-permute-start.54 = (bf16[48,2304]{1,0:T(8,128)(2,1)S(1)}, bf16[48,2304]{1,0:T(8,128)(2,1)S(1)}, u32[]{:S(2)}, u32[]{:S(2)}) collective-permute-start(bf16[48,2304]{1,0:T(8,128)(2,1)S(1)} %get-tuple-element.138), channel_id=1, source_target_pairs={{0,16},{2,18},{4,20},{6,22},{8,24},{10,26},{12,28},{14,30},{16,0},... | collective-permute-start | bytes 663560 | tf_op jit(solution)/shard_map/ppermute | solution.py:820
  442.6 18.9 %collective-permute-start.56 = (bf16[192,2304]{1,0:T(8,128)(2,1)S(1)}, bf16[192,2304]{1,0:T(8,128)(2,1)S(1)}, u32[]{:S(2)}, u32[]{:S(2)}) collective-permute-start(bf16[192,2304]{1,0:T(8,128)(2,1)S(1)} %pad_maximum_fusion.3), channel_id=1, source_target_pairs={{0,4},{2,6},{4,0},{6,2},{8,12},{10,14},{12,8},{14,10},{16,20},{18,... | collective-permute-start | bytes 2654216 | tf_op jit(solution)/shard_map/ppermute | solution.py:825
  531.4 22.3 %collective-permute-start.59 = (bf16[48,2304]{1,0:T(8,128)(2,1)S(1)}, bf16[48,2304]{1,0:T(8,128)(2,1)S(1)}, u32[]{:S(2)}, u32[]{:S(2)}) collective-permute-start(bf16[48,2304]{1,0:T(8,128)(2,1)S(1)} %get-tuple-element.133), channel_id=1, source_target_pairs={{0,16},{2,18},{4,20},{6,22},{8,24},{10,26},{12,28},{14,30},{16,0},... | collective-permute-start | bytes 663560 | tf_op jit(solution)/shard_map/ppermute | solution.py:831
  534.3 19.4 %collective-permute-start.58 = (bf16[48,2304]{1,0:T(8,128)(2,1)S(1)}, bf16[48,2304]{1,0:T(8,128)(2,1)S(1)}, u32[]{:S(2)}, u32[]{:S(2)}) collective-permute-start(bf16[48,2304]{1,0:T(8,128)(2,1)S(1)} %get-tuple-element.134), channel_id=1, source_target_pairs={{0,24},{2,26},{4,28},{6,30},{8,0},{10,2},{12,4},{14,6},{16,8},{18,... | collective-permute-start | bytes 663560 | tf_op jit(solution)/shard_map/ppermute | solution.py:831
  (146 other events, 2979.4 us)

commit v2 on v1

--- a/solution.py
+++ b/solution.py
@@ -463,40 +463,395 @@
     return first + second
 
 
-def place_rows(pieces, indices, widths):
+def dot_nn(left, right):
+    return lax.dot_general(
+        left, right, (((1,), (0,)), ((), ())), preferred_element_type=jnp.float32
+    )
+
+
+def lane_iota(shape):
+    return lax.broadcasted_iota(jnp.int32, shape, len(shape) - 1)
+
+
+def turn_lanes(field, head_size):
+    size = field.shape[-1]
+    half = head_size // 2
+    up = pltpu.roll(field, size - half, field.ndim - 1)
+    down = pltpu.roll(field, half, field.ndim - 1)
+    return jnp.where(lane_iota(field.shape) % head_size < half, up, down)
+
+
+def repeat_lanes(table, count):
+    return jnp.concatenate([table] * count, axis=1)
+
+
+def whole_spec():
+    return pl.BlockSpec(memory_space=pltpu.VMEM)
+
+
+def run_whole(body, index_row, inputs, outputs, scratch=()):
+    return pl.pallas_call(
+        body,
+        in_specs=[pl.BlockSpec(memory_space=pltpu.SMEM)] + [whole_spec()] * len(inputs),
+        out_specs=[whole_spec()] * len(outputs),
+        out_shape=[jax.ShapeDtypeStruct(shape, dtype) for shape, dtype in outputs],
+        scratch_shapes=list(scratch),
+        compiler_params=pltpu.CompilerParams(vmem_limit_bytes=56 * 1024 * 1024),
+    )(index_row, *inputs)
+
+
+def attend_stage(plan, index_row, own_pack, other_pack, cosine, sine, starts, pieces):
+    bf16, f32 = jnp.bfloat16, jnp.float32
+    tok, length, width, span, head_size = plan
     count = len(pieces)
     rows = pieces[0].shape[0]
-    offsets = [sum(widths[:k]) for k in range(len(widths))]
-
-    def body(*refs):
-        index_ref = refs[0]
-        piece_refs = refs[1 : 1 + count]
-        out_refs = refs[1 + count : 1 + count + len(widths)]
-        sems = refs[-1]
-        copies = []
+    score_scale = 1.0 / math.sqrt(head_size)
+    start_col = starts[:, None]
+    start_row = starts[None, :]
+
+    def body(index_ref, own_ref, other_ref, cos_ref, sin_ref, col_ref, row_ref, *rest):
+        piece_refs = rest[:count]
+        x_ref, dy_ref, a_ref, q_ref, k_ref, v_ref, o_ref, ob_ref, lse_ref, g_ref, w_ref = rest[
+            count : count + 11
+        ]
+        gain_ref = rest[-1]
+        half_at = index_ref[count]
+        own_at = pl.multiple_of(half_at * tok, tok)
+        other_at = pl.multiple_of((1 - half_at) * tok, tok)
+        x_ref[pl.ds(own_at, tok), :] = own_ref[:tok, :]
+        x_ref[pl.ds(other_at, tok), :] = other_ref[:tok, :]
+        dy_ref[pl.ds(own_at, tok), :] = own_ref[tok : 2 * tok, :]
+        dy_ref[pl.ds(other_at, tok), :] = other_ref[tok : 2 * tok, :]
         for piece_at in range(count):
-            start = pl.multiple_of(index_ref[piece_at] * rows, rows)
-            for width_at, width in enumerate(widths):
-                source = piece_refs[piece_at].at[:, pl.ds(offsets[width_at], width)]
-                target = out_refs[width_at].at[pl.ds(start, rows), :]
-                copies.append(
-                    pltpu.make_async_copy(source, target, sems.at[piece_at, width_at])
+            at = pl.ds(pl.multiple_of(index_ref[piece_at] * rows, rows), rows)
+            w_ref[at, :] = piece_refs[piece_at][:, : 3 * span]
+            gain_ref[at, :] = piece_refs[piece_at][:, 3 * span :].astype(f32)
+        gain_rows = jnp.transpose(gain_ref[...])
+        g_ref[...] = gain_rows[:8]
+        hat, _ = normalize(x_ref[...].astype(f32))
+        act = (hat * gain_rows[:1]).astype(bf16)
+        a_ref[...] = act
+        cos_wide = repeat_lanes(cos_ref[...], span // 128)
+        sin_wide = repeat_lanes(sin_ref[...], span // 128)
+        queries = dot_nn(act, w_ref[:, :span])
+        q_ref[...] = (queries * cos_wide + turn_lanes(queries, head_size) * sin_wide).astype(bf16)
+        keys = dot_nn(act, w_ref[:, span : 2 * span])
+        k_ref[...] = (keys * cos_wide + turn_lanes(keys, head_size) * sin_wide).astype(bf16)
+        v_ref[...] = dot_nn(act, w_ref[:, 2 * span :]).astype(bf16)
+        same = col_ref[...] == row_ref[...]
+        low = lane_iota((length, 128)) < head_size
+        lanes = lane_iota((length, 128))
+        logs = jnp.zeros((length, 128), f32)
+        for pair in range(span // 128):
+            cols = slice(pair * 128, pair * 128 + 128)
+            query, key, value = q_ref[:, cols], k_ref[:, cols], v_ref[:, cols]
+            parts = []
+            for side in range(2):
+                mine = low if side == 0 else jnp.logical_not(low)
+                score = contract_cols(jnp.where(mine, query, 0), key) * score_scale
+                weight = jnp.where(same, jnp.exp(score), 0.0)
+                total = jnp.sum(weight, axis=1, keepdims=True)
+                parts.append(dot_nn(weight.astype(bf16), value) / total)
+                logs = jnp.where(lanes == 2 * pair + side, jnp.log(total), logs)
+            mixed = jnp.where(low, parts[0], parts[1])
+            o_ref[:, cols] = mixed
+            ob_ref[:, cols] = mixed.astype(bf16)
+        lse_ref[...] = logs
+
+    return run_whole(
+        body,
+        index_row,
+        [own_pack, other_pack, cosine, sine, start_col, start_row, *pieces],
+        [
+            ((length, width), bf16),
+            ((length, width), bf16),
+            ((length, width), bf16),
+            ((length, span), bf16),
+            ((length, span), bf16),
+            ((length, span), bf16),
+            ((length, span), f32),
+            ((length, span), bf16),
+            ((length, 128), f32),
+            ((8, width), f32),
+            ((width, 3 * span), bf16),
+        ],
+        [pltpu.VMEM((width, 128), f32)],
+    )
+
+
+def lift_stage(plan, index_row, x, dy, own_mixed, other_mixed, gains, pieces):
+    bf16, f32 = jnp.bfloat16, jnp.float32
+    tok, length, width, span, units, core_units = plan
+    count = len(pieces)
+    rows = pieces[0].shape[0]
+    rest_units = units - core_units
+
+    def body(index_ref, x_ref, dy_ref, own_ref, other_ref, g_ref, *rest):
+        piece_refs = rest[:count]
+        (
+            wo_ref,
+            wm_ref,
+            h_ref,
+            hat_ref,
+            r_ref,
+            a_ref,
+            z_ref,
+            dp_ref,
+            dg_ref,
+            part_ref,
+            send_ref,
+        ) = rest[count : count + 11]
+        wp_ref, wg_ref = rest[-2:]
+        half_at = index_ref[count]
+        low = lane_iota((rows, 128)) < rest_units
+        zero = jnp.zeros((rows, 128), bf16)
+        edge = width + 3 * core_units
+        for piece_at in range(count):
+            at = pl.ds(pl.multiple_of(index_ref[piece_at] * rows, rows), rows)
+            piece = piece_refs[piece_at]
+            wo_ref[at, :] = piece[:, :width]
+            wp_ref[at, :core_units] = piece[:, width : width + core_units]
+            wg_ref[at, :core_units] = piece[:, width + core_units : width + 2 * core_units]
+            wm_ref[at, :core_units] = piece[:, width + 2 * core_units : edge]
+            both = piece[:, edge : edge + 128]
+            wp_ref[at, core_units:] = jnp.where(low, both, zero)
+            turned = pltpu.roll(both.astype(f32), 128 - rest_units, 1).astype(bf16)
+            wg_ref[at, core_units:] = jnp.where(low, turned, zero)
+            wm_ref[at, core_units:] = piece[:, edge + 128 : edge + 256]
+        own_at = pl.multiple_of(half_at * span, span)
+        other_at = pl.multiple_of((1 - half_at) * span, span)
+        hidden = (
+            x_ref[...].astype(f32)
+            + dot_nn(own_ref[...], wo_ref[pl.ds(own_at, span), :])
+            + dot_nn(other_ref[...], wo_ref[pl.ds(other_at, span), :])
+        )
+        h_ref[...] = hidden
+        hat, factor = normalize(hidden)
+        hat_ref[...] = hat
+        r_ref[...] = jnp.broadcast_to(factor, r_ref.shape)
+        act = (hat * g_ref[1:2, :]).astype(bf16)
+        a_ref[...] = act
+        preact = dot_nn(act, wp_ref[...])
+        gate = dot_nn(act, wg_ref[...])
+        activated, derivative = gelu_parts(preact)
+        z_ref[...] = (activated * gate).astype(bf16)
+        grad_inner = dot_nn(dy_ref[...], wm_ref[...])
+        grad_pre = (grad_inner * gate * derivative).astype(bf16)
+        grad_gate = (grad_inner * activated).astype(bf16)
+        dp_ref[...] = grad_pre
+        dg_ref[...] = grad_gate
+        part = contract_cols(grad_pre, wp_ref[...]) + contract_cols(grad_gate, wg_ref[...])
+        part_ref[...] = part
+        send_ref[...] = part.astype(bf16)
+
+    wide = core_units + 128
+    return run_whole(
+        body,
+        index_row,
+        [x, dy, own_mixed, other_mixed, gains, *pieces],
+        [
+            ((width, width), bf16),
+            ((width, wide), bf16),
+            ((length, width), f32),
+            ((length, width), f32),
+            ((length, 128), f32),
+            ((length, width), bf16),
+            ((length, wide), bf16),
+            ((length, wide), bf16),
+            ((length, wide), bf16),
+            ((length, width), f32),
+            ((length, width), bf16),
+        ],
+        [pltpu.VMEM((width, wide), bf16), pltpu.VMEM((width, wide), bf16)],
+    )
+
+
+def deal_rows(index_ref, base, core_at, rows, chips, scratch_ref, kept_ref, given_ref):
+    for step in range(chips):
+        chip = index_ref[base + step]
+        kept_at = pl.multiple_of((2 * chip + core_at) * rows, rows)
+        given_at = pl.multiple_of((2 * chip + 1 - core_at) * rows, rows)
+        kept_ref[step] = scratch_ref[pl.ds(kept_at, rows), :].astype(kept_ref.dtype)
+        given_ref[step] = scratch_ref[pl.ds(given_at, rows), :].astype(given_ref.dtype)
+
+
+def early_stage(plan, index_row, dy, act, inner, grad_pre, grad_gate, w_mlp, hidden, part, hat):
+    bf16, f32 = jnp.bfloat16, jnp.float32
+    tok, length, width, units, core_units, chips, rows = plan
+    rest_units = units - core_units
+    columns = 3 * core_units + 256
+    count = 2 * chips
+
+    def body(index_ref, dy_ref, a_ref, z_ref, dp_ref, dg_ref, wm_ref, h_ref, part_ref, hat_ref, *rest):
+        kept_ref, given_ref, out_ref, send_ref, gg_ref, whole_ref = rest
+        half_at = index_ref[count]
+        core_at = index_ref[count + 1]
+        grad_pre_w = contract_rows(a_ref[...], dp_ref[...])
+        whole_ref[:, :core_units] = grad_pre_w[:, :core_units]
+        grad_gate_w = contract_rows(a_ref[...], dg_ref[...])
+        whole_ref[:, core_units : 2 * core_units] = grad_gate_w[:, :core_units]
+        low = lane_iota((width, 128)) < rest_units
+        turned = pltpu.roll(grad_gate_w[:, core_units:], rest_units, 1)
+        whole_ref[:, 3 * core_units : 3 * core_units + 128] = jnp.where(
+            low, grad_pre_w[:, core_units:], turned
+        )
+        grad_mlp = contract_rows(dy_ref[...], z_ref[...])
+        whole_ref[:, 2 * core_units : 3 * core_units] = grad_mlp[:, :core_units]
+        whole_ref[:, 3 * core_units + 128 :] = grad_mlp[:, core_units:]
+        deal_rows(index_ref, count + 2, core_at, rows, chips, whole_ref, kept_ref, given_ref)
+        own_at = pl.multiple_of(half_at * tok, tok)
+        other_at = pl.multiple_of((1 - half_at) * tok, tok)
+        out_ref[...] = h_ref[pl.ds(own_at, tok), :] + contract_cols(
+            z_ref[pl.ds(own_at, tok), :], wm_ref[...]
+        )
+        send_ref[...] = contract_cols(z_ref[pl.ds(other_at, tok), :], wm_ref[...]).astype(bf16)
+        gg = jnp.sum(part_ref[...] * hat_ref[...], axis=0, keepdims=True)
+        gg_ref[...] = jnp.broadcast_to(gg, gg_ref.shape)
+
+    return run_whole(
+        body,
+        index_row,
+        [dy, act, inner, grad_pre, grad_gate, w_mlp, hidden, part, hat],
+        [
+            ((chips, rows, columns), bf16),
+            ((chips, rows, columns), bf16),
+            ((tok, width), f32),
+            ((tok, width), bf16),
+            ((8, width), f32),
+        ],
+        [pltpu.VMEM((width, columns), f32)],
+    )
+
+
+def late_stage(plan, index_row, inputs):
+    bf16, f32 = jnp.bfloat16, jnp.float32
+    tok, length, width, span, head_size, chips, rows = plan
+    score_scale = 1.0 / math.sqrt(head_size)
+    columns = 4 * span + 128
+    count = 2 * chips
+
+    def body(index_ref, *refs):
+        (
+            part_ref,
+            other_part_ref,
+            hat_ref,
+            r_ref,
+            dy_ref,
+            g_ref,
+            gg_ref,
+            wo_ref,
+            wq_ref,
+            x_ref,
+            a_ref,
+            q_ref,
+            k_ref,
+            v_ref,
+            o_ref,
+            lse_ref,
+            cos_ref,
+            sin_ref,
+            col_ref,
+            row_ref,
+            own_ref,
+            other_ref,
+            kept_ref,
+            given_ref,
+            dh_ref,
+            da_ref,
+            send_ref,
+            whole_ref,
+            do_ref,
+            dqkv_ref,
+        ) = refs
+        half_at = index_ref[count]
+        core_at = index_ref[count + 1]
+        gain_one = g_ref[0:1, :]
+        gain_two = g_ref[1:2, :]
+        grad_act = part_ref[...] + other_part_ref[...].astype(f32)
+        grad_hidden = dy_ref[...].astype(f32) + normalize_back(
+            grad_act * gain_two, hat_ref[...], r_ref[:, 0:1]
+        )
+        grad_b = grad_hidden.astype(bf16)
+        own_span = pl.multiple_of(half_at * span, span)
+        other_span = pl.multiple_of((1 - half_at) * span, span)
+        own_tok = pl.multiple_of(half_at * tok, tok)
+        other_tok = pl.multiple_of((1 - half_at) * tok, tok)
+        do_ref[...] = contract_cols(grad_b, wo_ref[pl.ds(own_span, span), :])
+        same = col_ref[...] == row_ref[...]
+        low = lane_iota((length, 128)) < head_size
+        cos, sin = cos_ref[...], sin_ref[...]
+        for pair in range(span // 128):
+            cols = slice(pair * 128, pair * 128 + 128)
+            query, key, value = q_ref[:, cols], k_ref[:, cols], v_ref[:, cols]
+            grad_o = do_ref[:, cols]
+            grad_ob = grad_o.astype(bf16)
+            product = grad_o * o_ref[:, cols]
+            found = []
+            for side in range(2):
+                head = 2 * pair + side
+                mine = low if side == 0 else jnp.logical_not(low)
+                delta = jnp.sum(jnp.where(mine, product, 0.0), axis=1, keepdims=True)
+                score = contract_cols(jnp.where(mine, query, 0), key) * score_scale
+                probs = jnp.where(same, jnp.exp(score - lse_ref[:, head : head + 1]), 0.0)
+                grad_probs = contract_cols(jnp.where(mine, grad_ob, 0), value)
+                grad_score = (probs * (grad_probs - delta)).astype(bf16)
+                found.append(
+                    (
+                        dot_nn(grad_score, key) * score_scale,
+                        contract_rows(grad_score, query) * score_scale,
+                        contract_rows(probs.astype(bf16), grad_ob),
+                    )
                 )
-        for copy in copies:
-            copy.start()
-        for copy in copies:
-            copy.wait()
-
-    anywhere = pl.BlockSpec(memory_space=pl.ANY)
-    return pl.pallas_call(
+            grad_q, grad_k, grad_v = (
+                jnp.where(low, even, odd) for even, odd in zip(found[0], found[1])
+            )
+            base = pair * 128
+            dqkv_ref[:, base : base + 128] = (
+                grad_q * cos - turn_lanes(grad_q, head_size) * sin
+            ).astype(bf16)
+            dqkv_ref[:, span + base : span + base + 128] = (
+                grad_k * cos - turn_lanes(grad_k, head_size) * sin
+            ).astype(bf16)
+            dqkv_ref[:, 2 * span + base : 2 * span + base + 128] = grad_v.astype(bf16)
+        whole_ref[:, : 3 * span] = contract_rows(a_ref[...], dqkv_ref[...])
+        half_b = jnp.where(half_at == 0, grad_hidden[:, :span], grad_hidden[:, span:]).astype(bf16)
+        whole_ref[pl.ds(own_span, span), 3 * span : 4 * span] = contract_rows(own_ref[...], half_b)
+        whole_ref[pl.ds(other_span, span), 3 * span : 4 * span] = contract_rows(
+            other_ref[...], half_b
+        )
+        grad_one = contract_cols(dqkv_ref[...], wq_ref[...])
+        hat_one, _ = normalize(x_ref[...].astype(f32))
+        gg_one = jnp.sum(grad_one * hat_one, axis=0, keepdims=True)
+        row_at = lax.broadcasted_iota(jnp.int32, (128, width), 0)
+        gain_rows = jnp.where(row_at == 0, gg_one, jnp.where(row_at == 1, gg_ref[0:1, :], 0.0))
+        whole_ref[:, 4 * span :] = jnp.transpose(gain_rows)
+        deal_rows(index_ref, count + 2, core_at, rows, chips, whole_ref, kept_ref, given_ref)
+        part_own = part_ref[pl.ds(own_tok, tok), :] + other_part_ref[pl.ds(own_tok, tok), :].astype(
+            f32
+        )
+        dh_ref[...] = dy_ref[pl.ds(own_tok, tok), :].astype(f32) + normalize_back(
+            part_own * gain_two, hat_ref[pl.ds(own_tok, tok), :], r_ref[pl.ds(own_tok, tok), 0:1]
+        )
+        da_ref[...] = contract_cols(dqkv_ref[pl.ds(own_tok, tok), :], wq_ref[...])
+        send_ref[...] = contract_cols(dqkv_ref[pl.ds(other_tok, tok), :], wq_ref[...]).astype(bf16)
+
+    return run_whole(
         body,
-        in_specs=[pl.BlockSpec(memory_space=pltpu.SMEM)] + [anywhere] * count,
-        out_specs=[anywhere] * len(widths),
-        out_shape=[
-            jax.ShapeDtypeStruct((count * rows, width), pieces[0].dtype) for width in widths
+        index_row,
+        inputs,
+        [
+            ((chips, rows, columns), bf16),
+            ((chips, rows, columns), bf16),
+            ((tok, width), f32),
+            ((tok, width), f32),
+            ((tok, width), bf16),
         ],
-        scratch_shapes=[pltpu.SemaphoreType.DMA((count, len(widths)))],
-    )(indices, *pieces)
+        [
+            pltpu.VMEM((width, columns), f32),
+            pltpu.VMEM((length, span), f32),
+            pltpu.VMEM((length, 3 * span), bf16),
+        ],
+    )
 
 
 def sweep_rows(start_rows, picked_rows):
@@ -563,8 +918,6 @@
     place = [0] * chip_count
     for spot, chip in enumerate(order):
         place[chip] = spot
-    order_table = jnp.array(order, jnp.int32)
-    spot_at = jnp.array(place, jnp.int32)[dp_at // 2]
 
     def ring_pairs(step):
         return [
@@ -578,9 +931,6 @@
     core_pairs = [(index, index ^ 1) for index in range(dp_count)]
     flip_pairs = [(0, 1), (1, 0)]
 
-    def chip_index(step):
-        return order_table[(spot_at + step + chip_count) % chip_count]
-
     def swap_core(value):
         return lax.ppermute(value, "dp", core_pairs)
 
@@ -590,51 +940,54 @@
     ahead_steps = chip_count // 2
     behind_steps = chip_count - 1 - ahead_steps
 
+    piece_steps = [0]
+    for step in range(1, ahead_steps + 1):
+        piece_steps.append(-step)
+        if step <= behind_steps:
+            piece_steps.append(step)
+
+    index_rows = []
+    for index in range(dp_count):
+        spot, core = place[index // 2], index % 2
+        chips_at = [order[(spot + step) % chip_count] for step in piece_steps]
+        ring_at = [order[(spot + step) % chip_count] for step in range(chip_count)]
+        for half in range(ctx_count):
+            row = [2 * chip + core for chip in chips_at] + [2 * chip + 1 - core for chip in chips_at]
+            index_rows.append(row + [half, core] + ring_at)
+    index_row = lax.dynamic_index_in_dim(
+        jnp.array(index_rows, jnp.int32), dp_at * ctx_count + half_at, 0, keepdims=False
+    )
+
     def ring_collect(shard):
-        steps = [0]
         pieces = [shard]
         ahead = shard
         behind = shard
         for step in range(1, ahead_steps + 1):
             ahead = lax.ppermute(ahead, "dp", forward_pairs)
-            steps.append(-step)
             pieces.append(ahead)
             if step <= behind_steps:
                 behind = lax.ppermute(behind, "dp", backward_pairs)
-                steps.append(step)
                 pieces.append(behind)
-        return steps, pieces
-
-    def collect(shard, widths):
-        steps, pieces = ring_collect(shard)
-        others = [swap_core(piece) for piece in pieces]
-        chips = jnp.stack([chip_index(step) for step in steps])
-        indices = jnp.concatenate([2 * chips + core_at, 2 * chips + 1 - core_at])
-        return place_rows(pieces + others, indices, widths)
-
-    def ring_reduce(partial):
-        columns = partial.shape[1]
-        split = partial.reshape(chip_count, 2, owned_rows, columns)
-        even, odd = split[:, 0], split[:, 1]
-        is_even = core_at == 0
-        kept = jnp.where(is_even, even, odd)
-        given = jnp.where(is_even, odd, even)
+        return pieces
+
+    def collect(shard):
+        pieces = ring_collect(shard)
+        return pieces + [swap_core(piece) for piece in pieces]
+
+    def ring_reduce(kept, given):
         chunks = (kept.astype(f32) + swap_core(given).astype(f32)).astype(bf16)
-
-        def chunk(step):
-            return lax.dynamic_index_in_dim(chunks, chip_index(step), 0, keepdims=False)
-
-        ahead = chunk(ahead_steps)
-        behind = chunk(-behind_steps)
+        ahead = chunks[ahead_steps]
+        behind = chunks[chip_count - behind_steps]
         for step in range(ahead_steps, 0, -1):
             ahead = lax.ppermute(ahead, "dp", forward_pairs)
             if step > 1:
-                ahead = (ahead.astype(f32) + chunk(step - 1).astype(f32)).astype(bf16)
+                ahead = (ahead.astype(f32) + chunks[step - 1].astype(f32)).astype(bf16)
             if step <= behind_steps:
                 behind = lax.ppermute(behind, "dp", backward_pairs)
                 if step > 1:
-                    behind = (behind.astype(f32) + chunk(1 - step).astype(f32)).astype(bf16)
-        return (chunk(0).astype(f32) + ahead.astype(f32) + behind.astype(f32)).astype(bf16)
+                    nearer = chunks[chip_count + 1 - step]
+                    behind = (behind.astype(f32) + nearer.astype(f32)).astype(bf16)
+        return (chunks[0].astype(f32) + ahead.astype(f32) + behind.astype(f32)).astype(bf16)
 
     def my_half(matrix, parts):
         rows = matrix.shape[0]
@@ -649,12 +1002,21 @@
 
     gain_columns = jnp.pad(jnp.transpose(norm_gains), ((0, 0), (0, 128 - norm_gains.shape[0])))
     first_shard = jnp.concatenate([my_half(w_qkv, 3), gain_columns], axis=1).astype(bf16)
-    pad_units = -hidden_half % 128
+    core_units = hidden_half // 128 * 128
+    rest_units = hidden_half - core_units
+    lift_h = my_half(w_in, 2)
+    lift_p, lift_g = lift_h[:, :hidden_half], lift_h[:, hidden_half:]
+    drop_h = my_half(w_mlp_out, 1)
     second_shard = jnp.concatenate(
         [
             w_attn_out,
-            my_half(w_in, 2),
-            jnp.pad(my_half(w_mlp_out, 1), ((0, 0), (0, pad_units))),
+            lift_p[:, :core_units],
+            lift_g[:, :core_units],
+            drop_h[:, :core_units],
+            lift_p[:, core_units:],
+            lift_g[:, core_units:],
+            drop_h[:, core_units:],
+            jnp.zeros((owned_rows, 128 - rest_units), f32),
         ],
         axis=1,
     ).astype(bf16)
@@ -664,117 +1026,100 @@
     digit_rows = jnp.pad(digits, ((0, 14), (0, width - tok_rows)))
     own_pack = jnp.concatenate([block_input[0], out_grad[0], digit_rows], axis=0)
     other_pack = swap_half(own_pack)
-    w_qkv_h, gains_t = collect(first_shard, (3 * span, 128))
-    w_out_b, w_in_h, w_mlp_p = collect(
-        second_shard, (width, 2 * hidden_half, hidden_half + pad_units)
-    )
-    w_mlp_h = w_mlp_p[:, :hidden_half]
+    first_pieces = collect(first_shard)
+    second_pieces = collect(second_shard)
 
     other_digits = other_pack[2 * tok_rows : 2 * tok_rows + 2, :tok_rows].astype(jnp.int32)
-    other_places = other_digits[0] * 128 + other_digits[1]
-    places = ordered(own_places, other_places, 0)
-    x_wide = ordered(own_pack[:tok_rows], other_pack[:tok_rows], 0).astype(f32)
-    dy_b = ordered(own_pack[tok_rows : 2 * tok_rows], other_pack[tok_rows : 2 * tok_rows], 0)
-    cosine, sine = rope_tables(places, head_size)
+    places = ordered(own_places, other_digits[0] * 128 + other_digits[1], 0)
+    lanes = jnp.arange(128, dtype=jnp.int32)
+    indices = (lanes % (head_size // 2)).astype(f32)
+    frequency = jnp.exp(indices * (-2.0 * math.log(theta_base) / head_size))
+    angles = places.astype(f32)[:, None] * frequency[None, :]
+    cosine = jnp.cos(angles)
+    sine = jnp.where((lanes % head_size < head_size // 2)[None, :], -1.0, 1.0) * jnp.sin(angles)
     starts = jnp.arange(length, dtype=jnp.int32) - places
-    same = (starts[:, None] == starts[None, :])[None]
-    gains_w = gains_t[:, :2].astype(f32)
-    gain_one = gains_w[:, 0]
-    gain_two = gains_w[:, 1]
-
-    hat_one, factor_one = normalize(x_wide)
-    act_one = (hat_one * gain_one).astype(bf16)
-    qkv = jnp.dot(act_one, w_qkv_h, preferred_element_type=f32)
-    queries_b = rotate(qkv[:, :span].reshape(length, heads, head_size), cosine, sine).astype(bf16)
-    keys_b = rotate(qkv[:, span : 2 * span].reshape(length, heads, head_size), cosine, sine).astype(
-        bf16
-    )
-    values_b = qkv[:, 2 * span :].astype(bf16).reshape(length, heads, head_size)
-    scores = (
-        jnp.einsum("qhd,khd->hqk", queries_b, keys_b, preferred_element_type=f32) * score_scale
-    )
-    weights = jnp.where(same, jnp.exp(scores), 0.0)
-    totals = jnp.sum(weights, axis=-1)
-    summed = jnp.einsum("hqk,khd->qhd", weights.astype(bf16), values_b, preferred_element_type=f32)
-    attended = summed / jnp.transpose(totals)[:, :, None]
-    log_total = jnp.log(totals)
-    own_mixed = attended.reshape(length, span).astype(bf16)
-    mixed_b = ordered(own_mixed, swap_half(own_mixed), 1)
-
-    hidden = x_wide + jnp.dot(mixed_b, w_out_b, preferred_element_type=f32)
-    hat_two, factor_two = normalize(hidden)
-    act_two = (hat_two * gain_two).astype(bf16)
-    lifted = jnp.dot(act_two, w_in_h, preferred_element_type=f32)
-    preact = lifted[:, :hidden_half]
-    gate_half = lifted[:, hidden_half:]
-    activated, derivative = gelu_parts(preact)
-    inner_b = (activated * gate_half).astype(bf16)
-    grad_inner = jnp.dot(dy_b, w_mlp_h, preferred_element_type=f32)
-    grad_lift = jnp.concatenate(
-        [grad_inner * gate_half * derivative, grad_inner * activated], axis=1
-    ).astype(bf16)
-    grad_two_part = contract_cols(grad_lift, w_in_h)
-    grad_act_two = grad_two_part + swap_half(grad_two_part.astype(bf16)).astype(f32)
-
-    def own_tokens(field):
-        return jnp.where(low_half, field[:tok_rows], field[tok_rows:])
-
-    def other_tokens(field):
-        return jnp.where(low_half, field[tok_rows:], field[:tok_rows])
-
-    out_part = contract_cols(inner_b, w_mlp_h)
-    output = (
-        own_tokens(hidden)
-        + own_tokens(out_part)
-        + swap_half(other_tokens(out_part).astype(bf16)).astype(f32)
-    )
-    grad_mlp = contract_rows(dy_b, inner_b)
-    grad_in = contract_rows(act_two, grad_lift)
-    early_rows = ring_reduce(jnp.concatenate([grad_in, grad_mlp], axis=1).astype(bf16))
-
-    gain_grad_two = jnp.sum(grad_two_part * hat_two, axis=0)
-    grad_hidden = dy_b.astype(f32) + normalize_back(grad_act_two * gain_two, hat_two, factor_two)
-    grad_hidden_b = grad_hidden.astype(bf16)
-    grad_out = contract_rows(
-        mixed_b, jnp.where(low_half, grad_hidden_b[:, :span], grad_hidden_b[:, span:])
-    )
-    out_rows_h = jnp.where(low_half, w_out_b[:span], w_out_b[span:])
-    grad_mixed = contract_cols(grad_hidden_b, out_rows_h).reshape(length, heads, head_size)
-    delta = jnp.sum(grad_mixed * attended, axis=-1)
-    grad_mixed_b = grad_mixed.astype(bf16)
-    probs = jnp.where(same, jnp.exp(scores - log_total[:, :, None]), 0.0)
-    grad_probs = jnp.einsum("qhd,khd->hqk", grad_mixed_b, values_b, preferred_element_type=f32)
-    grad_scores_b = (probs * (grad_probs - jnp.transpose(delta)[:, :, None])).astype(bf16)
-    query_grad = (
-        jnp.einsum("hqk,khd->qhd", grad_scores_b, keys_b, preferred_element_type=f32) * score_scale
-    )
-    key_grad = (
-        jnp.einsum("hqk,qhd->khd", grad_scores_b, queries_b, preferred_element_type=f32)
-        * score_scale
-    )
-    value_grad = jnp.einsum(
-        "hqk,qhd->khd", probs.astype(bf16), grad_mixed_b, preferred_element_type=f32
-    )
-    grad_qkv_in = jnp.concatenate(
+
+    x, dy, act_one, queries, keys, values, mixed, own_mixed, logs, gains, w_qkv_h = attend_stage(
+        (tok_rows, length, width, span, head_size),
+        index_row,
+        own_pack,
+        other_pack,
+        cosine,
+        sine,
+        starts,
+        first_pieces,
+    )
+    other_mixed = swap_half(own_mixed)
+    (
+        w_out_b,
+        w_mlp_h,
+        hidden,
+        hat_two,
+        factor_two,
+        act_two,
+        inner,
+        grad_pre,
+        grad_gate,
+        grad_two_part,
+        grad_two_send,
+    ) = lift_stage(
+        (tok_rows, length, width, span, hidden_half, core_units),
+        index_row,
+        x,
+        dy,
+        own_mixed,
+        other_mixed,
+        gains,
+        second_pieces,
+    )
+    other_two_part = swap_half(grad_two_send)
+    early_kept, early_given, out_own, out_send, gain_two_grad = early_stage(
+        (tok_rows, length, width, hidden_half, core_units, chip_count, owned_rows),
+        index_row,
+        dy,
+        act_two,
+        inner,
+        grad_pre,
+        grad_gate,
+        w_mlp_h,
+        hidden,
+        grad_two_part,
+        hat_two,
+    )
+    early_rows = ring_reduce(early_kept, early_given)
+    output = out_own + swap_half(out_send).astype(f32)
+    late_kept, late_given, grad_hidden_own, grad_one_own, grad_one_send = late_stage(
+        (tok_rows, length, width, span, head_size, chip_count, owned_rows),
+        index_row,
         [
-            rotate_back(query_grad, cosine, sine).reshape(length, span),
-            rotate_back(key_grad, cosine, sine).reshape(length, span),
-            value_grad.reshape(length, span),
+            grad_two_part,
+            other_two_part,
+            hat_two,
+            factor_two,
+            dy,
+            gains,
+            gain_two_grad,
+            w_out_b,
+            w_qkv_h,
+            x,
+            act_one,
+            queries,
+            keys,
+            values,
+            mixed,
+            logs,
+            cosine,
+            sine,
+            starts[:, None],
+            starts[None, :],
+            own_mixed,
+            other_mixed,
         ],
-        axis=1,
-    ).astype(bf16)
-    grad_qkv = contract_rows(act_one, grad_qkv_in)
-    grad_one_part = contract_cols(grad_qkv_in, w_qkv_h)
-    gain_grad_one = jnp.sum(grad_one_part * hat_one, axis=0)
-    gain_pair = jnp.pad(jnp.stack([gain_grad_one, gain_grad_two], axis=1), ((0, 0), (0, 126)))
-    late_rows = ring_reduce(jnp.concatenate([grad_qkv, grad_out, gain_pair], axis=1).astype(bf16))
-
-    grad_act_one = own_tokens(grad_one_part) + swap_half(
-        other_tokens(grad_one_part).astype(bf16)
-    ).astype(f32)
-    grad_input = own_tokens(grad_hidden) + normalize_back(
-        grad_act_one * gain_one, own_tokens(hat_one), own_tokens(factor_one)
-    )
+    )
+    late_rows = ring_reduce(late_kept, late_given)
+    grad_act_one = grad_one_own + swap_half(grad_one_send).astype(f32)
+    hat_own, factor_own = normalize(block_input[0].astype(f32))
+    grad_input = grad_hidden_own + normalize_back(grad_act_one * gains[0], hat_own, factor_own)
 
     def whole_columns(own, other, parts):
         rows = own.shape[0]
@@ -783,8 +1128,24 @@
         return jnp.stack([first, second], axis=2).reshape(rows, -1).astype(f32)
 
     factor = 1.0 / math.sqrt(dp_count * length)
-    early_other = swap_half(early_rows)
     late_other = swap_half(late_rows)
+
+    def unpacked(rows):
+        edge = 3 * core_units
+        return jnp.concatenate(
+            [
+                rows[:, :core_units],
+                rows[:, edge : edge + rest_units],
+                rows[:, core_units : 2 * core_units],
+                rows[:, edge + rest_units : edge + 2 * rest_units],
+                rows[:, 2 * core_units : edge],
+                rows[:, edge + 128 : edge + 128 + rest_units],
+            ],
+            axis=1,
+        )
+
+    early_other = unpacked(swap_half(early_rows))
+    early_rows = unpacked(early_rows)
     cut = 2 * hidden_half
     grads = [
         whole_columns(late_rows[:, : 3 * span], late_other[:, : 3 * span], 3) * factor,
@@ -855,7 +1216,7 @@
 
 def fits_pairs(mesh):
     dp_count, ctx_count = mesh.shape["dp"], mesh.shape["ctx"]
-    return ctx_count == 2 and HEADS % 2 == 0 and dp_count % 8 == 0
+    return ctx_count == 2 and HEADS % 4 == 0 and dp_count % 8 == 0
 
 
 def solution(mesh):

time: 564 us -> 290 us (0.51); the launches traced: 556 us -> 292 us
  Pallas kernels: 183 us -> 41.6 us
  local copies, waits for them, and re-layouts: 58.9 us -> 20.7 us
  other arithmetic: 43.5 us -> 19.5 us
  between operations: 25.1 us -> 2.88 us
  matrix products: 74.3 us -> 54.7 us
  waiting for transfers between devices: 123 us -> 104 us
    pallas_call x2 -> x4, Pallas kernels: 183 us -> 41.6 us  [run_whole(): pl.pallas_call(body, in_specs=[pl.BlockSpec(memory_space=pltpu.SMEM)] + [...]
    ppermute x8, waiting for transfers between devices: 44.4 us -> 17.1 us  [ring_reduce(): ahead = lax.ppermute(ahead, 'dp', forward_pairs)]
    dot_general x14 -> x0, matrix products: 14.6 us -> none  [the longest x4 5.65 us: contract_rows(): lax.dot_general(left_side, right_side, (((0,), (0,)), ((), ())), preferre...]
    unnamed x230 -> x132, local copies, waits for them, and re-layouts: 21 us -> 8.32 us
    ppermute x7, waiting for transfers between devices: 16.2 us -> 27.5 us  [swap_half(): return lax.ppermute(value, 'ctx', flip_pairs)]
    ppermute x2 -> x0, local copies, waits for them, and re-layouts: 9.37 us -> none  [swap_core(): return lax.ppermute(value, 'dp', core_pairs)]
    select_n x3 -> x4, local copies, waits for them, and re-layouts: 8.94 us -> 0.36 us  [the longest x2 0.18 us: whole_columns(): first = jnp.where(low_half, own, other).reshape(rows, parts, -1)]
    convert_element_type x2, other arithmetic: 9 us -> 0.63 us  [ring_reduce(): chunks = (kept.astype(f32) + swap_core(given).astype(f32)).astype(bf16)]
  transfers between devices with their start and end apart: 61 -> 61, of which waited for: 22 -> 31; matrix products, arithmetic and copies ran while one was open for 18% -> 9% of each run, Pallas kernels for 11% -> 10%
where the time goes in v2:
time: 290 us; the launch traced here: 292 us
  waiting for transfers between devices  104 us (36%)
  matrix products  54.7 us (19%)
  starting transfers between devices  48.3 us (17%)
  Pallas kernels  41.6 us (14%)
  local copies, waits for them, and re-layouts  20.7 us (7%)
  other arithmetic  19.5 us (7%)
    pallas_call x4, Pallas kernels, run_whole(): pl.pallas_call(body, in_specs=[pl.BlockSpec(memory_space=pltpu.SMEM)] + [...  41.6 us
    ppermute x7, waiting for transfers between devices, swap_half(): return lax.ppermute(value, 'ctx', flip_pairs)  27.5 us
    ppermute x8, waiting for transfers between devices, ring_reduce(): ahead = lax.ppermute(ahead, 'dp', forward_pairs)  17.1 us
    ppermute x3, waiting for transfers between devices, paired_device(): returned.append(lax.ppermute(turned[step], 'dp', shift_pairs(-step)))  16.3 us
    ppermute x1, waiting for transfers between devices, paired_device(): held = jnp.concatenate([held, lax.ppermute(held, 'dp', pairs)], axis=0)  15.6 us
    dot_general x4, matrix products, sweep_rows(): jnp.dot(jnp.dot(gram, factor, precision=high), factor, precision=high)  13.3 us
    dot_general x4, matrix products, sweep_rows(): square = jnp.dot(gram, gram, precision=high)  13.1 us
    ppermute x8, waiting for transfers between devices, ring_collect(): ahead = lax.ppermute(ahead, 'dp', forward_pairs)  12.9 us
  transfers between devices with their start and end apart: 61, of which 31 were waited for; matrix products, arithmetic and copies ran while one was open for 9% of the time, Pallas kernels for 10%

profile of v2, /device:TPU:26, one launch (start us, length us, event | category | flops | bytes accessed | tf_op | source)
XLA Modules:
  0.0 291.6 jit_solution(1846295030836526375)
XLA Ops:
  11.4 3.5 %collective-permute-done.4.rest_4_ = bf16[48,1280]{1,0:T(8,128)(2,1)S(1)} collective-permute-done((bf16[48,1280]{1,0:T(8,128)(2,1)S(1)}, bf16[48,1280]{1,0:T(8,128)(2,1)S(1)}, u32[]{:S(2)}, u32[]{:S(2)}) %collective-permute-start.4) | collective-permute-done | bytes 122912 | tf_op jit(solution)/shard_map/ppermute | solution.py:969
  20.2 3.7 %collective-permute-done.3.rest_3_ = bf16[48,1280]{1,0:T(8,128)(2,1)S(1)} collective-permute-done((bf16[48,1280]{1,0:T(8,128)(2,1)S(1)}, bf16[48,1280]{1,0:T(8,128)(2,1)S(1)}, u32[]{:S(2)}, u32[]{:S(2)}) %collective-permute-start.3) | collective-permute-done | bytes 122912 | tf_op jit(solution)/shard_map/ppermute | solution.py:966
  44.1 5.0 %shard_map.286 = (bf16[256,768]{1,0:T(8,128)(2,1)}, bf16[256,768]{1,0:T(8,128)(2,1)}, bf16[256,768]{1,0:T(8,128)(2,1)}, bf16[256,384]{1,0:T(8,128)(2,1)}, bf16[2...) custom-call(s32[26]{0:T(128)} %fusion.113.index_ref, ...), custom_call_target="tpu_custom_call" | custom-call | tf_op jit(solution)/shard_map/pallas_call | solution.py:493
  49.7 7.0 %collective-permute-done.16.other_ref.refs_21_ = bf16[256,384]{1,0:T(8,128)(2,1)S(1)} collective-permute-done((bf16[256,384]{1,0:T(8,128)(2,1)}, bf16[256,384]{1,0:T(8,128)(2,1)S(1)}, u32[]{:S(2)}, u32[]{:S(2)}) %collective-permute-start.16) | collective-permute-done | bytes 196640 | tf_op jit(solution)/shard_map/ppermute | solution.py:938
  57.7 6.9 %shard_map.287 = (bf16[768,768]{1,0:T(8,128)(2,1)}, bf16[768,640]{1,0:T(8,128)(2,1)}, f32[256,768]{1,0:T(8,128)}, f32[256,768]{1,0:T(8,128)}, f32[256,128]{1,0:T...) custom-call(s32[26]{0:T(128)} %fusion.113.index_ref, ...), custom_call_target="tpu_custom_call" | custom-call | tf_op jit(solution)/shard_map/pallas_call | solution.py:493
  64.7 5.9 %shard_map.288 = (bf16[8,48,1792]{2,1,0:T(8,128)(2,1)}, bf16[8,48,1792]{2,1,0:T(8,128)(2,1)}, f32[128,768]{1,0:T(8,128)}, bf16[128,768]{1,0:T(8,128)(2,1)}, f32[8,768]{1,0:T(8,128)}) custom-call(s32[26]{0:T(128)} %fusion.113.index_ref, bf16[256,768]{1,0:T(8,128)(2,1)} %get-tuple-element.50.dy_ref.refs_4_, bf16[256,768]{1,0:T(8,128)(2,1)} %get-tuple-element.54.a_ref, ...), custom_call_target="tpu_custom_call" | custom-call | tf_op jit(solution)/shard_map/pallas_call | solution.py:493
  72.4 9.7 %collective-permute-done.33.refs_1_ = bf16[256,768]{1,0:T(8,128)(2,1)S(1)} collective-permute-done((bf16[256,768]{1,0:T(8,128)(2,1)S(1)}, bf16[256,768]{1,0:T(8,128)(2,1)S(1)}, u32[]{:S(2)}, u32[]{:S(2)}) %collective-permute-start.33) | collective-permute-done | bytes 393248 | tf_op jit(solution)/shard_map/ppermute | solution.py:938
  82.9 23.8 %shard_map.289 = (bf16[8,48,1664]{2,1,0:T(8,128)(2,1)}, bf16[8,48,1664]{2,1,0:T(8,128)(2,1)}, f32[128,768]{1,0:T(8,128)}, f32[128,768]{1,0:T(8,128)}, bf16[128,768]{1,0:T(8,128)(2,1)}) custom-call(s32[26]{0:T(128)} %fusion.113.index_ref, f32[256,768]{1,0:T(8,128)} %get-tuple-element.60.part_ref.refs_0_, bf16[256,768]{1,0:T(8,128)(2,1)} %copy-done.22, ...), custom_call_target="tpu_custom_call" | custom-call | tf_op jit(solution)/shard_map/pallas_call | solution.py:493
  109.2 4.7 %collective-permute-done.45 = bf16[48,1792]{1,0:T(8,128)(2,1)S(1)} collective-permute-done((bf16[48,1792]{1,0:T(8,128)(2,1)S(1)}, bf16[48,1792]{1,0:T(8,128)(2,1)S(1)}, u32[]{:S(2)}, u32[]{:S(2)}) %collective-permute-start.45) | collective-permute-done | bytes 172064 | tf_op jit(solution)/shard_map/ppermute | solution.py:982
  116.9 4.4 %collective-permute-done.46 = bf16[48,1792]{1,0:T(8,128)(2,1)S(1)} collective-permute-done((bf16[48,1792]{1,0:T(8,128)(2,1)S(1)}, bf16[48,1792]{1,0:T(8,128)(2,1)S(1)}, u32[]{:S(2)}, u32[]{:S(2)}) %collective-permute-start.46) | collective-permute-done | bytes 172064 | tf_op jit(solution)/shard_map/ppermute | solution.py:982
  125.2 3.4 %collective-permute-done.47 = bf16[48,1792]{1,0:T(8,128)(2,1)S(1)} collective-permute-done((bf16[48,1792]{1,0:T(8,128)(2,1)S(1)}, bf16[48,1792]{1,0:T(8,128)(2,1)S(1)}, u32[]{:S(2)}, u32[]{:S(2)}) %collective-permute-start.47) | collective-permute-done | bytes 172064 | tf_op jit(solution)/shard_map/ppermute | solution.py:982
  147.7 4.4 %collective-permute-done.43 = bf16[48,1664]{1,0:T(8,128)(2,1)S(1)} collective-permute-done((bf16[48,1664]{1,0:T(8,128)(2,1)S(1)}, bf16[48,1664]{1,0:T(8,128)(2,1)S(1)}, u32[]{:S(2)}, u32[]{:S(2)}) %collective-permute-start.43) | collective-permute-done | bytes 159776 | tf_op jit(solution)/shard_map/ppermute | solution.py:938
  160.2 4.2 %collective-permute-done.55 = bf16[48,2304]{1,0:T(8,128)(2,1)S(1)} collective-permute-done((bf16[48,2304]{1,0:T(8,128)(2,1)S(1)}, bf16[48,2304]{1,0:T(8,128)(2,1)S(1)}, u32[]{:S(2)}, u32[]{:S(2)}) %collective-permute-start.55) | collective-permute-done | bytes 221216 | tf_op jit(solution)/shard_map/ppermute | solution.py:1181
  164.5 4.9 %collective-permute-done.54 = bf16[48,2304]{1,0:T(8,128)(2,1)S(1)} collective-permute-done((bf16[48,2304]{1,0:T(8,128)(2,1)S(1)}, bf16[48,2304]{1,0:T(8,128)(2,1)S(1)}, u32[]{:S(2)}, u32[]{:S(2)}) %collective-permute-start.54) | collective-permute-done | bytes 221216 | tf_op jit(solution)/shard_map/ppermute | solution.py:1181
  173.6 15.6 %collective-permute-done.56 = bf16[192,2304]{1,0:T(8,128)(2,1)S(1)} collective-permute-done((bf16[192,2304]{1,0:T(8,128)(2,1)S(1)}, bf16[192,2304]{1,0:T(8,128)(2,1)S(1)}, u32[]{:S(2)}, u32[]{:S(2)}) %collective-permute-start.56) | collective-permute-done | bytes 884768 | tf_op jit(solution)/shard_map/ppermute | solution.py:1186
  199.0 3.8 %collective-permute-done.34 = bf16[128,768]{1,0:T(8,128)(2,1)S(1)} collective-permute-done((bf16[128,768]{1,0:T(8,128)(2,1)}, bf16[128,768]{1,0:T(8,128)(2,1)S(1)}, u32[]{:S(2)}, u32[]{:S(2)}) %collective-permute-start.34) | collective-permute-done | bytes 196640 | tf_op jit(solution)/shard_map/ppermute | solution.py:938
  207.4 6.6 %select_reduce_fusion = (f32[]{:T(128)}, f32[768,768]{1,0:T(8,128)S(1)}) fusion(bf16[768,2304]{1,0:T(8,128)(2,1)} %constant_dynamic-update-slice_fusion.5), kind=kOutput, calls=%fused_computation.11 | convolution fusion | flops 2719678464 | bytes 5898244 | tf_op jit(solution)/shard_map/dot_general | solution.py:91
  221.2 3.6 %fusion.158 = f32[768,768]{1,0:T(8,128)S(1)} fusion(f32[768,768]{1,0:T(8,128)S(1)} %fusion.4, f32[768,768]{1,0:T(8,128)S(1)} %fusion), kind=kOutput, calls=%fused_computation.279 | convolution fusion | flops 2717908992 | bytes 7077888 | tf_op jit(solution)/shard_map/dot_general | solution.py:878
  232.4 3.2 %fusion.22 = f32[768,768]{1,0:T(8,128)S(1)} fusion(f32[768,768]{1,0:T(8,128)S(1)} %fusion.24, f32[768,768]{1,0:T(8,128)S(1)} %fusion.159, f32[768,768]{1,0:T(8,128)S(1)} %fusion.158), kind=kOutput, calls=%fused_computation.23 | convolution fusion | flops 2721447936 | bytes 9437184 | tf_op jit(solution)/shard_map/dot_general | solution.py:878
  235.6 3.3 %fusion.160 = f32[768,768]{1,0:T(8,128)S(1)} fusion(f32[768,768]{1,0:T(8,128)S(1)} %fusion.22), kind=kOutput, calls=%fused_computation.281 | convolution fusion | flops 2717908992 | bytes 4718592 | tf_op jit(solution)/shard_map/dot_general | solution.py:871
  246.7 3.4 %fusion.161 = f32[768,768]{1,0:T(8,128)S(1)} fusion(f32[768,768]{1,0:T(8,128)S(1)} %fusion.16), kind=kOutput, calls=%fused_computation.282 | convolution fusion | flops 2717908992 | bytes 4718592 | tf_op jit(solution)/shard_map/dot_general | solution.py:871
  263.1 3.5 %collective-permute-start.60 = (bf16[48,2304]{1,0:T(8,128)(2,1)S(1)}, bf16[48,2304]{1,0:T(8,128)(2,1)S(1)}, u32[]{:S(2)}, u32[]{:S(2)}) collective-permute-start(bf16[48,2304]{1,0:T(8,128)(2,1)S(1)} %get-tuple-element.222), channel_id=1, source_target_pairs={{0,8},{2,10},{4,12},{6,14},{8,16},{10,18},{12,20},{14,22},{16,24},... | collective-permute-start | bytes 663560 | tf_op jit(solution)/shard_map/ppermute | solution.py:1192
  266.7 3.3 %collective-permute-start.59 = (bf16[48,2304]{1,0:T(8,128)(2,1)S(1)}, bf16[48,2304]{1,0:T(8,128)(2,1)S(1)}, u32[]{:S(2)}, u32[]{:S(2)}) collective-permute-start(bf16[48,2304]{1,0:T(8,128)(2,1)S(1)} %get-tuple-element.223), channel_id=1, source_target_pairs={{0,16},{2,18},{4,20},{6,22},{8,24},{10,26},{12,28},{14,30},{16,0},... | collective-permute-start | bytes 663560 | tf_op jit(solution)/shard_map/ppermute | solution.py:1192
  273.4 15.4 %collective-permute-done.59 = bf16[48,2304]{1,0:T(8,128)(2,1)S(1)} collective-permute-done((bf16[48,2304]{1,0:T(8,128)(2,1)S(1)}, bf16[48,2304]{1,0:T(8,128)(2,1)S(1)}, u32[]{:S(2)}, u32[]{:S(2)}) %collective-permute-start.59) | collective-permute-done | bytes 221216 | tf_op jit(solution)/shard_map/ppermute | solution.py:1192
  (360 shorter events, 135.5 us)
Async XLA Ops:
  5.4 14.3 %collective-permute-start = (bf16[272,768]{1,0:T(8,128)(2,1)S(1)}, bf16[272,768]{1,0:T(8,128)(2,1)S(1)}, u32[]{:S(2)}, u32[]{:S(2)}) collective-permute-start(bf16[272,768]{1,0:T(8,128)(2,1)S(1)} %pad_maximum_fusion.3.own_ref), channel_id=1, source_target_pairs={{0,1},{1,0},{2,3},{3,2},{4,5},{5,4},{6,7},{7,6},{8,9},{9,8},{10,11... | collective-permute-start | bytes 1253384 | tf_op jit(solution)/shard_map/ppermute | solution.py:938
  8.7 9.5 %collective-permute-start.17 = (bf16[48,2560]{1,0:T(8,128)(2,1)S(1)}, bf16[48,2560]{1,0:T(8,128)(2,1)S(1)}, u32[]{:S(2)}, u32[]{:S(2)}) collective-permute-start(bf16[48,2560]{1,0:T(8,128)(2,1)S(1)} %concatenate.108.rest_0_), channel_id=1, source_target_pairs={{0,8},{2,10},{8,16},{10,18},{16,24},{18,26},{24,28},{26,30},{28,20... | collective-permute-start | bytes 737288 | tf_op jit(solution)/shard_map/ppermute | solution.py:966
  11.0 12.9 %collective-permute-start.24 = (bf16[48,2560]{1,0:T(8,128)(2,1)S(1)}, bf16[48,2560]{1,0:T(8,128)(2,1)S(1)}, u32[]{:S(2)}, u32[]{:S(2)}) collective-permute-start(bf16[48,2560]{1,0:T(8,128)(2,1)S(1)} %concatenate.108.rest_0_), channel_id=1, source_target_pairs={{0,2},{2,0},{4,6},{6,4},{8,10},{10,8},{12,14},{14,12},{16,18},{18,... | collective-permute-start | bytes 737288 | tf_op jit(solution)/shard_map/ppermute | solution.py:935
  14.9 9.5 %collective-permute-start.18 = (bf16[48,2560]{1,0:T(8,128)(2,1)S(1)}, bf16[48,2560]{1,0:T(8,128)(2,1)S(1)}, u32[]{:S(2)}, u32[]{:S(2)}) collective-permute-start(bf16[48,2560]{1,0:T(8,128)(2,1)S(1)} %concatenate.108.rest_0_), channel_id=1, source_target_pairs={{0,4},{2,6},{8,0},{10,2},{16,8},{18,10},{24,16},{26,18},{28,24},{3... | collective-permute-start | bytes 737288 | tf_op jit(solution)/shard_map/ppermute | solution.py:969
  28.2 8.6 %collective-permute-start.21 = (bf16[48,2560]{1,0:T(8,128)(2,1)S(1)}, bf16[48,2560]{1,0:T(8,128)(2,1)S(1)}, u32[]{:S(2)}, u32[]{:S(2)}) collective-permute-start(bf16[48,2560]{1,0:T(8,128)(2,1)S(1)} %collective-permute-done.19.rest_3_), channel_id=1, source_target_pairs={{0,8},{2,10},{8,16},{10,18},{16,24},{18,26},{24,28},{26,30},{28,20... | collective-permute-start | bytes 737288 | tf_op jit(solution)/shard_map/ppermute | solution.py:966
  28.7 10.3 %collective-permute-start.26 = (bf16[48,2560]{1,0:T(8,128)(2,1)S(1)}, bf16[48,2560]{1,0:T(8,128)(2,1)S(1)}, u32[]{:S(2)}, u32[]{:S(2)}) collective-permute-start(bf16[48,2560]{1,0:T(8,128)(2,1)S(1)} %collective-permute-done.18.rest_2_), channel_id=1, source_target_pairs={{0,2},{2,0},{4,6},{6,4},{8,10},{10,8},{12,14},{14,12},{16,18},{18,... | collective-permute-start | bytes 737288 | tf_op jit(solution)/shard_map/ppermute | solution.py:935
  39.0 10.1 %collective-permute-start.28 = (bf16[48,2560]{1,0:T(8,128)(2,1)S(1)}, bf16[48,2560]{1,0:T(8,128)(2,1)S(1)}, u32[]{:S(2)}, u32[]{:S(2)}) collective-permute-start(bf16[48,2560]{1,0:T(8,128)(2,1)S(1)} %collective-permute-done.20.rest_4_), channel_id=1, source_target_pairs={{0,2},{2,0},{4,6},{6,4},{8,10},{10,8},{12,14},{14,12},{16,18},{18,... | collective-permute-start | bytes 737288 | tf_op jit(solution)/shard_map/ppermute | solution.py:935
  40.2 9.5 %collective-permute-start.27 = (bf16[48,2560]{1,0:T(8,128)(2,1)S(1)}, bf16[48,2560]{1,0:T(8,128)(2,1)S(1)}, u32[]{:S(2)}, u32[]{:S(2)}) collective-permute-start(bf16[48,2560]{1,0:T(8,128)(2,1)S(1)} %collective-permute-done.19.rest_3_), channel_id=1, source_target_pairs={{0,2},{2,0},{4,6},{6,4},{8,10},{10,8},{12,14},{14,12},{16,18},{18,... | collective-permute-start | bytes 737288 | tf_op jit(solution)/shard_map/ppermute | solution.py:935
  40.7 16.1 %collective-permute-start.29 = (bf16[48,2560]{1,0:T(8,128)(2,1)S(1)}, bf16[48,2560]{1,0:T(8,128)(2,1)S(1)}, u32[]{:S(2)}, u32[]{:S(2)}) collective-permute-start(bf16[48,2560]{1,0:T(8,128)(2,1)S(1)} %collective-permute-done.21.rest_5_), channel_id=1, source_target_pairs={{0,2},{2,0},{4,6},{6,4},{8,10},{10,8},{12,14},{14,12},{16,18},{18,... | collective-permute-start | bytes 737288 | tf_op jit(solution)/shard_map/ppermute | solution.py:935
  41.2 15.5 %collective-permute-start.30 = (bf16[48,2560]{1,0:T(8,128)(2,1)S(1)}, bf16[48,2560]{1,0:T(8,128)(2,1)S(1)}, u32[]{:S(2)}, u32[]{:S(2)}) collective-permute-start(bf16[48,2560]{1,0:T(8,128)(2,1)S(1)} %collective-permute-done.22.rest_6_), channel_id=1, source_target_pairs={{0,2},{2,0},{4,6},{6,4},{8,10},{10,8},{12,14},{14,12},{16,18},{18,... | collective-permute-start | bytes 737288 | tf_op jit(solution)/shard_map/ppermute | solution.py:935
  43.6 13.2 %collective-permute-start.31 = (bf16[48,2560]{1,0:T(8,128)(2,1)}, bf16[48,2560]{1,0:T(8,128)(2,1)S(1)}, u32[]{:S(2)}, u32[]{:S(2)}) collective-permute-start(bf16[48,2560]{1,0:T(8,128)(2,1)} %collective-permute-done.23.rest_7_), channel_id=1, source_target_pairs={{0,2},{2,0},{4,6},{6,4},{8,10},{10,8},{12,14},{14,12},{16,18},{18,... | collective-permute-start | bytes 737288 | tf_op jit(solution)/shard_map/ppermute | solution.py:935
  70.6 36.1 %collective-permute-start.44 = (bf16[8,48,1792]{2,1,0:T(8,128)(2,1)}, bf16[8,48,1792]{2,1,0:T(8,128)(2,1)S(1)}, u32[]{:S(2)}, u32[]{:S(2)}) collective-permute-start(bf16[8,48,1792]{2,1,0:T(8,128)(2,1)} %get-tuple-element.81), channel_id=1, source_target_pairs={{0,2},{2,0},{4,6},{6,4},{8,10},{10,8},{12,14},{14,12},{16,18},{18,... | collective-permute-start | bytes 4128776 | tf_op jit(solution)/shard_map/ppermute | solution.py:935
  70.6 11.5 %collective-permute-start.33 = (bf16[256,768]{1,0:T(8,128)(2,1)S(1)}, bf16[256,768]{1,0:T(8,128)(2,1)S(1)}, u32[]{:S(2)}, u32[]{:S(2)}) collective-permute-start(bf16[256,768]{1,0:T(8,128)(2,1)S(1)} %copy-done.59), channel_id=1, source_target_pairs={{0,1},{1,0},{2,3},{3,2},{4,5},{5,4},{6,7},{7,6},{8,9},{9,8},{10,11... | collective-permute-start | bytes 1179656 | tf_op jit(solution)/shard_map/ppermute | solution.py:938
  107.6 9.3 %collective-permute-start.49 = (bf16[48,1792]{1,0:T(8,128)(2,1)S(1)}, bf16[48,1792]{1,0:T(8,128)(2,1)S(1)}, u32[]{:S(2)}, u32[]{:S(2)}) collective-permute-start(bf16[48,1792]{1,0:T(8,128)(2,1)S(1)} %get-tuple-element.210), channel_id=1, source_target_pairs={{0,4},{2,6},{8,0},{10,2},{16,8},{18,10},{24,16},{26,18},{28,24},{3... | collective-permute-start | bytes 516104 | tf_op jit(solution)/shard_map/ppermute | solution.py:986
  114.8 9.9 %collective-permute-start.36 = (bf16[48,1664]{1,0:T(8,128)(2,1)S(1)}, bf16[48,1664]{1,0:T(8,128)(2,1)S(1)}, u32[]{:S(2)}, u32[]{:S(2)}) collective-permute-start(bf16[48,1664]{1,0:T(8,128)(2,1)S(1)} %get-tuple-element.215), channel_id=1, source_target_pairs={{0,8},{2,10},{8,16},{10,18},{16,24},{18,26},{24,28},{26,30},{28,20... | collective-permute-start | bytes 479240 | tf_op jit(solution)/shard_map/ppermute | solution.py:982
  115.3 15.5 %collective-permute-start.40 = (bf16[48,1664]{1,0:T(8,128)(2,1)S(1)}, bf16[48,1664]{1,0:T(8,128)(2,1)S(1)}, u32[]{:S(2)}, u32[]{:S(2)}) collective-permute-start(bf16[48,1664]{1,0:T(8,128)(2,1)S(1)} %get-tuple-element.216), channel_id=1, source_target_pairs={{0,4},{2,6},{8,0},{10,2},{16,8},{18,10},{24,16},{26,18},{28,24},{3... | collective-permute-start | bytes 479240 | tf_op jit(solution)/shard_map/ppermute | solution.py:986
  155.0 9.5 %collective-permute-start.55 = (bf16[48,2304]{1,0:T(8,128)(2,1)S(1)}, bf16[48,2304]{1,0:T(8,128)(2,1)S(1)}, u32[]{:S(2)}, u32[]{:S(2)}) collective-permute-start(bf16[48,2304]{1,0:T(8,128)(2,1)S(1)} %get-tuple-element.227), channel_id=1, source_target_pairs={{0,24},{2,26},{4,28},{6,30},{8,0},{10,2},{12,4},{14,6},{16,8},{18,... | collective-permute-start | bytes 663560 | tf_op jit(solution)/shard_map/ppermute | solution.py:1181
  155.4 14.0 %collective-permute-start.54 = (bf16[48,2304]{1,0:T(8,128)(2,1)S(1)}, bf16[48,2304]{1,0:T(8,128)(2,1)S(1)}, u32[]{:S(2)}, u32[]{:S(2)}) collective-permute-start(bf16[48,2304]{1,0:T(8,128)(2,1)S(1)} %get-tuple-element.228), channel_id=1, source_target_pairs={{0,16},{2,18},{4,20},{6,22},{8,24},{10,26},{12,28},{14,30},{16,0},... | collective-permute-start | bytes 663560 | tf_op jit(solution)/shard_map/ppermute | solution.py:1181
  156.1 13.4 %collective-permute-start.53 = (bf16[48,2304]{1,0:T(8,128)(2,1)S(1)}, bf16[48,2304]{1,0:T(8,128)(2,1)S(1)}, u32[]{:S(2)}, u32[]{:S(2)}) collective-permute-start(bf16[48,2304]{1,0:T(8,128)(2,1)S(1)} %get-tuple-element.229), channel_id=1, source_target_pairs={{0,8},{2,10},{4,12},{6,14},{8,16},{10,18},{12,20},{14,22},{16,24},... | collective-permute-start | bytes 663560 | tf_op jit(solution)/shard_map/ppermute | solution.py:1181
  169.5 19.7 %collective-permute-start.56 = (bf16[192,2304]{1,0:T(8,128)(2,1)S(1)}, bf16[192,2304]{1,0:T(8,128)(2,1)S(1)}, u32[]{:S(2)}, u32[]{:S(2)}) collective-permute-start(bf16[192,2304]{1,0:T(8,128)(2,1)S(1)} %pad_maximum_fusion.1), channel_id=1, source_target_pairs={{0,4},{2,6},{4,0},{6,2},{8,12},{10,14},{12,8},{14,10},{16,20},{18,... | collective-permute-start | bytes 2654216 | tf_op jit(solution)/shard_map/ppermute | solution.py:1186
  190.5 15.5 %collective-permute-start.57 = (bf16[384,2304]{1,0:T(8,128)(2,1)}, bf16[384,2304]{1,0:T(8,128)(2,1)S(1)}, u32[]{:S(2)}, u32[]{:S(2)}) collective-permute-start(bf16[384,2304]{1,0:T(8,128)(2,1)} %get-tuple-element.225), channel_id=1, source_target_pairs={{0,2},{2,0},{4,6},{6,4},{8,10},{10,8},{12,14},{14,12},{16,18},{18,... | collective-permute-start | bytes 5308424 | tf_op jit(solution)/shard_map/ppermute | solution.py:935
  263.1 10.3 %collective-permute-start.60 = (bf16[48,2304]{1,0:T(8,128)(2,1)S(1)}, bf16[48,2304]{1,0:T(8,128)(2,1)S(1)}, u32[]{:S(2)}, u32[]{:S(2)}) collective-permute-start(bf16[48,2304]{1,0:T(8,128)(2,1)S(1)} %get-tuple-element.222), channel_id=1, source_target_pairs={{0,8},{2,10},{4,12},{6,14},{8,16},{10,18},{12,20},{14,22},{16,24},... | collective-permute-start | bytes 663560 | tf_op jit(solution)/shard_map/ppermute | solution.py:1192
  266.7 22.2 %collective-permute-start.59 = (bf16[48,2304]{1,0:T(8,128)(2,1)S(1)}, bf16[48,2304]{1,0:T(8,128)(2,1)S(1)}, u32[]{:S(2)}, u32[]{:S(2)}) collective-permute-start(bf16[48,2304]{1,0:T(8,128)(2,1)S(1)} %get-tuple-element.223), channel_id=1, source_target_pairs={{0,16},{2,18},{4,20},{6,22},{8,24},{10,26},{12,28},{14,30},{16,0},... | collective-permute-start | bytes 663560 | tf_op jit(solution)/shard_map/ppermute | solution.py:1192
  269.9 18.9 %collective-permute-start.58 = (bf16[48,2304]{1,0:T(8,128)(2,1)S(1)}, bf16[48,2304]{1,0:T(8,128)(2,1)S(1)}, u32[]{:S(2)}, u32[]{:S(2)}) collective-permute-start(bf16[48,2304]{1,0:T(8,128)(2,1)S(1)} %get-tuple-element.224), channel_id=1, source_target_pairs={{0,24},{2,26},{4,28},{6,30},{8,0},{10,2},{12,4},{14,6},{16,8},{18,... | collective-permute-start | bytes 663560 | tf_op jit(solution)/shard_map/ppermute | solution.py:1192
  (97 other events, 1027.4 us)
